TPU v7x, 128 devices: a whole 4x4x4 slice. The times are simulated.
128 devices in a mesh: ctx: 16 (over x, y), fsdp: 8 (over z, core).
Axes of the slice: x: 4, y: 4, z: 4, core: 2. Of those that a mesh axis runs over, the one named last changes fastest.
Arguments:
- tokens: bfloat16 [16384, 4096], P(('ctx', 'fsdp')), may hold values from -360 to 360
- norm_gain: float32 [4096], replicated, may hold values from 0.1 to 1.9
- qkv_weight: bfloat16 [3, 4096, 2048], P(None, 'ctx', 'fsdp'), may hold values from -1 to 1
- out_weight: bfloat16 [2048, 4096], P('fsdp', 'ctx'), may hold values from -1 to 1
- layout: int32 [128, 16], replicated, may hold values from 0 to 127, as said below
Outputs:
- branch_out: bfloat16 [16384, 4096], P(('ctx', 'fsdp'))
Inputs may be any that keep to these rules, and one draw needn't show every extreme that they name: `layout`: every entry of query block i names a block of 0 to i. With the blocks taken in spans of 8, the query blocks of one span name at most 2 distinct blocks of any other span, and some pair of spans reaches 2 in every draw.
All inputs are finite; a program needn't handle non-finite values.
Results may differ from a plain program's by a relative error of at most 0.015.
Values may be sent and summed in bfloat16 or wider, within the bound.
A program may use at most 128 MiB of HBM per device.

v0:
```python
import math

import jax
import jax.numpy as jnp
from jax import lax
from jax.sharding import PartitionSpec as P

HEAD_DIM = 128
BLK = 128
SUMMARY = 16


EPSILON = 1e-05


def normalize(tokens, norm_gain):
    features = tokens.astype(jnp.float32)
    mean_square = jnp.mean(features * features, axis=-1, keepdims=True)
    return (features * lax.rsqrt(mean_square + EPSILON) * norm_gain).astype(jnp.bfloat16)


def shards(tokens, norm_gain, qkv_weight, out_weight, layout):
    normed = normalize(tokens, norm_gain)
    gathered = lax.all_gather(normed, "fsdp", axis=0, tiled=True)
    span_rows = gathered.shape[0]
    local_width = qkv_weight.shape[2]
    heads_here = local_width // HEAD_DIM
    projected = jnp.einsum(
        "td,cdi->cti",
        gathered,
        lax.all_gather(qkv_weight, "ctx", axis=1, tiled=True),
        preferred_element_type=jnp.float32,
    ).astype(jnp.bfloat16)
    queries, key_rows, value_rows = (projected[0], projected[1], projected[2])
    ctx_index = lax.axis_index("ctx")
    span_blocks = span_rows // BLK
    key_slots = 2 + SUMMARY
    first_block = ctx_index * span_blocks
    own_blocks = first_block + jnp.arange(span_blocks, dtype=jnp.int32)
    listed = lax.dynamic_slice_in_dim(layout, first_block, span_blocks, 0)
    key_index = jnp.concatenate([own_blocks[:, None], own_blocks[:, None] - 1, listed], axis=1)
    every_key, every_value = (
        lax.all_gather(key_rows, "ctx", axis=0, tiled=True),
        lax.all_gather(value_rows, "ctx", axis=0, tiled=True),
    )
    total_blocks = every_key.shape[0] // BLK
    pool_keys = every_key.reshape(total_blocks, BLK, local_width)
    pool_values = every_value.reshape(total_blocks, BLK, local_width)
    gather_index = jnp.maximum(key_index, 0)
    group_size = math.gcd(span_blocks, max(1, 512 // BLK))
    group_count = span_blocks // group_size
    score_scale = HEAD_DIM ** (-0.5)
    offsets = jnp.arange(BLK, dtype=jnp.int32)

    def attend(packed):
        group_queries, group_index, group_slots, group_blocks = packed
        key_blocks = pool_keys[group_index].reshape(
            group_size, key_slots, BLK, heads_here, HEAD_DIM
        )
        value_blocks = pool_values[group_index].reshape(
            group_size, key_slots, BLK, heads_here, HEAD_DIM
        )
        scores = (
            jnp.einsum(
                "bqhd,bnkhd->bhqnk", group_queries, key_blocks, preferred_element_type=jnp.float32
            )
            * score_scale
        )
        query_pos = group_blocks[:, None] * BLK + offsets[None, :]
        key_pos = group_slots[:, :, None] * BLK + offsets[None, None, :]
        allowed = (key_pos[:, None, :, :] <= query_pos[:, :, None, None]) & (
            key_pos[:, None, :, :] >= 0
        )
        allowed = allowed[:, None]
        scores = jnp.where(allowed, scores, -1e30)
        row_max = jnp.max(scores, axis=(3, 4), keepdims=True)
        weights = jnp.where(allowed, jnp.exp(scores - row_max), 0.0)
        denominator = jnp.sum(weights, axis=(3, 4), keepdims=True)
        weights = (weights / denominator).astype(jnp.bfloat16)
        blended = jnp.einsum(
            "bhqnk,bnkhd->bqhd", weights, value_blocks, preferred_element_type=jnp.float32
        )
        return blended.astype(jnp.bfloat16)

    packed_inputs = (
        queries.reshape(group_count, group_size, BLK, heads_here, HEAD_DIM),
        gather_index.reshape(group_count, group_size, key_slots),
        key_index.reshape(group_count, group_size, key_slots),
        own_blocks.reshape(group_count, group_size),
    )
    blended_all = lax.map(attend, packed_inputs)
    attended = blended_all.reshape(span_rows, local_width)
    projection = lax.all_gather(out_weight, "ctx", axis=1, tiled=True)
    return lax.psum_scatter(
        jnp.dot(attended, projection, preferred_element_type=jnp.float32).astype(jnp.bfloat16),
        "fsdp",
        scatter_dimension=0,
        tiled=True,
    )


def solution(mesh):
    placed = (P(("ctx", "fsdp"), None), P(), P(None, "ctx", "fsdp"), P("fsdp", "ctx"), P())
    return jax.shard_map(
        shards, mesh=mesh, in_specs=placed, out_specs=P(("ctx", "fsdp"), None), check_vma=False
    )
```

profile of v0, /device:TPU:30, one launch (start us, length us, event | category | flops | bytes accessed | tf_op | source)
XLA Modules:
  0.0 462.8 jit_solution(6775085235407852516)
XLA Ops:
  6.5 0.7 all-gather.10.cloned.1.call-update
  7.3 1.5 fusion.24
  8.8 2.5 fusion.26
  11.4 59.4 %all-gather.10.cloned.1.call-done = bf16[3,4096,256]{2,1,0:T(8,128)(2,1)} async-done(((bf16[3,256,256]{2,1,0:T(8,128)(2,1)}), bf16[3,4096,256]{2,1,0:T(8,128)(2,1)}) %all-gather.10.cloned.1.call-update) | async-done | bytes 6291472 | tf_op jit(solution)/shard_map/all_gather | solution.py:31
  70.8 53.2 %all-gather.8.cloned.1.call-done = bf16[1024,4096]{1,0:T(8,128)(2,1)} async-done(((bf16[128,4096]{1,0:T(8,128)(2,1)}), bf16[1024,4096]{1,0:T(8,128)(2,1)}) %all-gather.8.cloned.1.call-update) | async-done | bytes 8388624 | tf_op jit(solution)/shard_map/all_gather | solution.py:24
  124.1 10.9 %fusion.30 = bf16[3,1024,256]{2,1,0:T(8,128)(2,1)S(1)} fusion(bf16[3,4096,256]{2,1,0:T(8,128)(2,1)} %all-gather.10.cloned.1.call-done, bf16[1024,4096]{1,0:T(8,128)(2,1)} %all-gather.8.cloned.1.call-done), kind=kOutput, calls=%fused_computation.40 | convolution fusion | flops 6443237376 | bytes 16252928 | tf_op jit(solution)/shard_map/td,cdi->cti/dot_general | solution.py:28
  135.0 1.1 fusion.35
  136.1 0.5 all-gather.16.cloned.1.call-update
  136.7 0.5 all-gather.12.cloned.1.call-update
  137.5 0.1 broadcast_maximum_fusion
  137.6 0.1 reshape_squeeze.3
  137.7 67.3 %all-gather.14.cloned.1.call-done = bf16[1,16384,256]{2,1,0:T(8,128)(2,1)} async-done(((bf16[1,1024,256]{2,1,0:T(8,128)(2,1)}), bf16[1,16384,256]{2,1,0:T(8,128)(2,1)}) %all-gather.14.cloned.1.call-update) | async-done | bytes 8388624 | tf_op jit(solution)/shard_map/all_gather | solution.py:44
  205.0 72.4 %all-gather.16.cloned.1.call-done = bf16[1,16384,256]{2,1,0:T(8,128)(2,1)} async-done(((bf16[1,1024,256]{2,1,0:T(8,128)(2,1)}), bf16[1,16384,256]{2,1,0:T(8,128)(2,1)}) %all-gather.16.cloned.1.call-update) | async-done | bytes 8388624 | tf_op jit(solution)/shard_map/all_gather | solution.py:43
  277.4 116.8 %while.12 = (s32[]{:T(128)}, bf16[2,4,128,2,128]{4,3,2,1,0:T(2,128)(2,1)S(1)}, s32[2,4,18]{2,1,0:T(4,128)S(1)}, bf16[128,128,256]{2,1,0:T(8,128)(2,1)}, s32[2,4,...) while((s32[]{:T(128)}, ...), condition=%wide.region_4.5_spmd.clone.clone, body=%wide.region_1.4_spmd.clone.clone.sunk | while | flops 1243507456 | bytes 139060496 | solution.py:91
  277.5 0.1 broadcast_compare_fusion.2
  277.7 3.5 compare_and_fusion.2
  281.2 0.1 reshape.195
  281.3 8.9 %gather_fusion = bf16[72,128,256]{2,1,0:T(8,128)(2,1)} fusion(bf16[128,128,256]{2,1,0:T(8,128)(2,1)} %get-tuple-element.209, s32[1024]{0:T(1024)S(1)} %pad_clamp_fusion.2), kind=kCustom, calls=%fused_computation.1.clone.clone.1 | custom fusion | bytes 9437472 | tf_op jit(solution)/shard_map/while/body/eval_jaxpr/gather | solution.py:57
  290.2 7.8 %reshape.196 = bf16[4,18,128,2,128]{4,3,2,1,0:T(2,128)(2,1)} reshape(bf16[72,128,256]{2,1,0:T(8,128)(2,1)} %gather_fusion) | data formatting | bytes 9437184 | tf_op jit(solution)/shard_map/while/body/eval_jaxpr/reshape | solution.py:57
  298.0 3.6 copy.44
  301.6 0.2 constant_dynamic-slice_fusion.4
  301.8 1.4 fusion.48
  303.2 1.6 fusion.50
  304.7 2.1 copy-done.2
  306.8 2.5 fusion.51
  309.3 9.0 %gather_fusion.1 = bf16[72,128,256]{2,1,0:T(8,128)(2,1)} fusion(bf16[128,128,256]{2,1,0:T(8,128)(2,1)} %get-tuple-element.205, s32[1024]{0:T(1024)S(1)} %pad_clamp_fusion.2), kind=kCustom, calls=%fused_computation.clone.clone.1 | custom fusion | bytes 9437472 | tf_op jit(solution)/shard_map/while/body/eval_jaxpr/gather | solution.py:60
  318.4 7.7 %reshape.197 = bf16[4,18,128,2,128]{4,3,2,1,0:T(2,128)(2,1)} reshape(bf16[72,128,256]{2,1,0:T(8,128)(2,1)} %gather_fusion.1) | data formatting | bytes 9437184 | tf_op jit(solution)/shard_map/while/body/eval_jaxpr/reshape | solution.py:60
  326.1 9.4 %fusion.52 = bf16[1,4,128,2,128]{2,4,3,1,0:T(8,128)(2,1)S(1)} fusion(f32[4,2,128,18,128]{2,4,3,1,0:T(8,128)} %bitcast.66, f32[4,2,128]{2,1,0:T(2,128)S(1)} %fusion.51, f32[4,2,128]{2,1,0:T(2,128)S(1)} %fusion.50, pred[4,128,18,128]{1,3,2,0:T(8,128)(4,1)S(1)} %compare_and_fusion.2, bf16[4,18,128,2,128]{4,3,2,1,0:T(2,128)(2,1)} %reshape.197), kind=kOutput, calls=%fused_computation.14.clone.1 | convolution fusion | flops 618266624 | bytes 15605760 | tf_op jit(solution)/shard_map/while/body/eval_jaxpr/bhqnk,bnkhd->bqhd/dot_general | solution.py:80
  335.5 0.2 copy.45
  335.7 0.2 constant_dynamic-update-slice_fusion.2
  336.0 0.1 broadcast_compare_fusion.2
  336.2 3.5 compare_and_fusion.2
  339.7 0.1 reshape.195
  339.8 8.9 %gather_fusion = bf16[72,128,256]{2,1,0:T(8,128)(2,1)} fusion(bf16[128,128,256]{2,1,0:T(8,128)(2,1)} %get-tuple-element.209, s32[1024]{0:T(1024)S(1)} %pad_clamp_fusion.2), kind=kCustom, calls=%fused_computation.1.clone.clone.1 | custom fusion | bytes 9437472 | tf_op jit(solution)/shard_map/while/body/eval_jaxpr/gather | solution.py:57
  348.6 7.7 %reshape.196 = bf16[4,18,128,2,128]{4,3,2,1,0:T(2,128)(2,1)} reshape(bf16[72,128,256]{2,1,0:T(8,128)(2,1)} %gather_fusion) | data formatting | bytes 9437184 | tf_op jit(solution)/shard_map/while/body/eval_jaxpr/reshape | solution.py:57
  356.4 3.6 copy.44
  359.9 0.2 constant_dynamic-slice_fusion.4
  360.1 1.4 fusion.48
  361.5 1.6 fusion.50
  363.1 2.1 copy-done.2
  365.2 2.5 fusion.51
  367.7 8.8 %gather_fusion.1 = bf16[72,128,256]{2,1,0:T(8,128)(2,1)} fusion(bf16[128,128,256]{2,1,0:T(8,128)(2,1)} %get-tuple-element.205, s32[1024]{0:T(1024)S(1)} %pad_clamp_fusion.2), kind=kCustom, calls=%fused_computation.clone.clone.1 | custom fusion | bytes 9437472 | tf_op jit(solution)/shard_map/while/body/eval_jaxpr/gather | solution.py:60
  376.5 7.7 %reshape.197 = bf16[4,18,128,2,128]{4,3,2,1,0:T(2,128)(2,1)} reshape(bf16[72,128,256]{2,1,0:T(8,128)(2,1)} %gather_fusion.1) | data formatting | bytes 9437184 | tf_op jit(solution)/shard_map/while/body/eval_jaxpr/reshape | solution.py:60
  384.3 9.4 %fusion.52 = bf16[1,4,128,2,128]{2,4,3,1,0:T(8,128)(2,1)S(1)} fusion(f32[4,2,128,18,128]{2,4,3,1,0:T(8,128)} %bitcast.66, f32[4,2,128]{2,1,0:T(2,128)S(1)} %fusion.51, f32[4,2,128]{2,1,0:T(2,128)S(1)} %fusion.50, pred[4,128,18,128]{1,3,2,0:T(8,128)(4,1)S(1)} %compare_and_fusion.2, bf16[4,18,128,2,128]{4,3,2,1,0:T(2,128)(2,1)} %reshape.197), kind=kOutput, calls=%fused_computation.14.clone.1 | convolution fusion | flops 618266624 | bytes 15605760 | tf_op jit(solution)/shard_map/while/body/eval_jaxpr/bhqnk,bnkhd->bqhd/dot_general | solution.py:80
  393.6 0.2 copy.45
  393.8 0.2 constant_dynamic-update-slice_fusion.2
  394.3 7.2 %convolution_convert_fusion = bf16[1024,4096]{1,0:T(8,128)(2,1)} fusion(bf16[256,4096]{1,0:T(8,128)(2,1)} %all-gather.12.cloned.1.call-done, bf16[128,8,2,128]{3,2,1,0:T(2,128)(2,1)S(1)} %bitcast.70), kind=kOutput, calls=%fused_computation.33 | convolution fusion | flops 2151677952 | bytes 11010048 | tf_op jit(solution)/shard_map/dot_general | solution.py:95
  401.5 54.4 %reduce-scatter.2.cloned.1.call-done = bf16[128,4096]{1,0:T(8,128)(2,1)} async-done(((bf16[1024,4096]{1,0:T(8,128)(2,1)}), bf16[128,4096]{1,0:T(8,128)(2,1)}) %reduce-scatter.2.cloned.1.call-update) | async-done | bytes 1048592 | tf_op jit(solution)/shard_map/reduce_scatter | solution.py:94
  (34 shorter events, 0.8 us)
Async XLA Ops:
  6.5 130.8 %copy-start = (s32[128,16]{0,1:T(8,128)S(1)}, s32[128,16]{0,1:T(8,128)}, u32[]{:S(2)}) copy-start(s32[128,16]{0,1:T(8,128)} %param.11) | copy-start | bytes 24580
  6.5 64.3 %all-gather.10.cloned.1.call-start = ((), (), s32[]{:S(2)}) async-start(), calls=%async_computation.2 | async-start | bytes 6684672 | tf_op jit(solution)/shard_map/all_gather | solution.py:31
  7.3 116.8 %all-gather.8.cloned.1.call-start = ((), (), s32[]{:S(2)}) async-start(), calls=%async_computation.1 | async-start | bytes 9437184 | tf_op jit(solution)/shard_map/all_gather | solution.py:24
  11.4 193.6 %all-gather.14.cloned.1.call-start = ((), (), s32[]{:S(2)}) async-start(), calls=%async_computation.5 | async-start | bytes 8912896 | tf_op jit(solution)/shard_map/all_gather | solution.py:44
  136.1 141.3 %all-gather.16.cloned.1.call-start = ((), (), s32[]{:S(2)}) async-start(), calls=%async_computation.6 | async-start | bytes 8912896 | tf_op jit(solution)/shard_map/all_gather | solution.py:43
  136.7 257.6 %all-gather.12.cloned.1.call-start = ((), (), s32[]{:S(2)}) async-start(), calls=%async_computation.3 | async-start | bytes 2228224 | tf_op jit(solution)/shard_map/all_gather | solution.py:93
  137.2 318.7 %reduce-scatter.2.cloned.1.call-start = ((), (), s32[]{:S(2)}) async-start(), calls=%async_computation.4 | async-start | bytes 9437184 | tf_op jit(solution)/shard_map/reduce_scatter | solution.py:94
  303.2 3.6 copy-start.2
  361.5 3.6 copy-start.2
  394.3 61.6 %copy-start.1 = (s32[128,16]{0,1:T(8,128)S(1)}, s32[128,16]{0,1:T(8,128)}, u32[]{:S(2)}) copy-start(s32[128,16]{0,1:T(8,128)} %param.11) | copy-start | bytes 24580
Sparse Core Ops, SparseCore 0:
  9.5 61.2 all-gather.9
  72.6 51.4 all-gather.7
  136.2 68.7 all-gather.13
  207.0 70.3 all-gather.15
  279.4 46.2 all-gather.11
  401.6 54.2 reduce-scatter.1
where the time goes:
time: 464 us; the launch traced here: 463 us
  waiting for transfers between devices  309 us (67%)
  local copies, waits for them, and re-layouts  80.5 us (17%)
  matrix products  39.6 us (9%)
  other arithmetic  19.8 us (4%)
  between operations  13.5 us (3%)
    all_gather x1, waiting for transfers between devices, shards(): lax.all_gather(key_rows, 'ctx', axis=0, tiled=True)  72.4 us
    all_gather x1, waiting for transfers between devices, shards(): lax.all_gather(value_rows, 'ctx', axis=0, tiled=True)  67.3 us
    all_gather x1, waiting for transfers between devices, shards(): lax.all_gather(qkv_weight, 'ctx', axis=1, tiled=True)  59.4 us
    reduce_scatter x1, waiting for transfers between devices, shards(): lax.psum_scatter(jnp.dot(attended, projection, preferred_element_type=jnp...  54.4 us
    all_gather x1, waiting for transfers between devices, shards(): gathered = lax.all_gather(normed, 'fsdp', axis=0, tiled=True)  53.2 us
    reshape x4, local copies, waits for them, and re-layouts, attend(): pool_keys[group_index]  22.7 us
    dot_general x2, matrix products, attend(): jnp.einsum('bhqnk,bnkhd->bqhd', weights, value_blocks, preferred_element_...  18.8 us
    gather x2, local copies, waits for them, and re-layouts, attend(): pool_values[group_index]  17.9 us
  transfers between devices with their start and end apart: 6, of which 5 were waited for; matrix products, arithmetic and copies ran while one was open for 25% of the time, Pallas kernels for 0%

commit v1 on v0

v1 whole, which is shorter than its diff:
```python
import functools

import jax
import jax.numpy as jnp
from jax import lax
from jax.experimental import pallas as pl
from jax.experimental.pallas import tpu as pltpu
from jax.sharding import PartitionSpec as P

HEAD_DIM = 128
BLK = 128
EPSILON = 1e-05
CAP = 2
MESH = pl.DeviceIdType.MESH


def normalize(tokens, norm_gain):
    features = tokens.astype(jnp.float32)
    mean_square = jnp.mean(features * features, axis=-1, keepdims=True)
    return (features * lax.rsqrt(mean_square + EPSILON) * norm_gain).astype(jnp.bfloat16)


def block_tables(layout, spans):
    me = lax.axis_index("ctx")
    blocks, listed = layout.shape
    own = blocks // spans
    entries = layout.reshape(spans, own * listed)
    home, within = entries // own, entries % own
    mine = home == me
    lowest = jnp.min(jnp.where(mine, within, own - 1), axis=1)
    highest = jnp.max(jnp.where(mine, within, 0), axis=1)
    pick = jnp.stack([lowest, highest], axis=1).reshape(-1)
    rows = lax.dynamic_index_in_dim(entries, me, 0, keepdims=False)
    row_home, row_within = rows // own, rows % own
    same = row_home[:, None] == row_home[None, :]
    low = jnp.min(jnp.where(same, row_within[None, :], own - 1), axis=1)
    far = own + CAP * row_home + jnp.where(row_within == low, 0, 1)
    listed_slot = jnp.where(row_home == me, row_within, far).reshape(own, listed)
    index = jnp.arange(own, dtype=jnp.int32)
    block = me * own + index
    before = jnp.where(index > 0, index - 1, jnp.where(me > 0, own + CAP * spans, 0))
    slot = jnp.concatenate([index[:, None], before[:, None], listed_slot], axis=1)
    gap = block[:, None] - rows.reshape(own, listed)
    before_gap = jnp.where(block > 0, 1, -1)
    reach = jnp.concatenate([jnp.zeros_like(index)[:, None], before_gap[:, None], gap], axis=1) * BLK
    return pick.astype(jnp.int32), slot.reshape(-1).astype(jnp.int32), reach.reshape(-1).astype(jnp.int32)


def attend_kernel(
    spans, slots, pick, slot, reach, q, k, v, out, kpool, vpool, kstage, vstage, scores, own_sem, send_sem, recv_sem
):
    me, lane = lax.axis_index("ctx"), lax.axis_index("fsdp")
    own = q.shape[0]
    heads = q.shape[2] // HEAD_DIM
    barrier = pltpu.get_barrier_semaphore()

    @pl.loop(1, spans)
    def _(step):
        peer = lax.rem(me + step, spans)
        pl.semaphore_signal(barrier, inc=1, device_id=(peer, lane), device_id_type=MESH)

    keep = [
        pltpu.make_async_copy(k, kpool.at[pl.ds(0, own)], own_sem.at[0]),
        pltpu.make_async_copy(v, vpool.at[pl.ds(0, own)], own_sem.at[1]),
    ]
    for copy in keep:
        copy.start()

    @pl.loop(0, spans * CAP)
    def _(n):
        kstage[n] = k[pick[n]]
        vstage[n] = v[pick[n]]

    pl.semaphore_wait(barrier, spans - 1)

    def listed(src, dst):
        there = pl.ds(own + CAP * src, CAP)
        return [
            pltpu.make_async_remote_copy(
                stage.at[pl.ds(CAP * dst, CAP)], pool.at[there],
                send_sem.at[dst, j], recv_sem.at[src, j], device_id=(dst, lane), device_id_type=MESH,
            )
            for j, (stage, pool) in enumerate(((kstage, kpool), (vstage, vpool)))
        ]

    def previous(dst):
        there = own + CAP * spans
        return [
            pltpu.make_async_remote_copy(
                mine.at[own - 1], pool.at[there],
                send_sem.at[spans, j], recv_sem.at[spans, j], device_id=(dst, lane), device_id_type=MESH,
            )
            for j, (mine, pool) in enumerate(((k, kpool), (v, vpool)))
        ]

    @pl.when(me < spans - 1)
    def _():
        for copy in previous(me + 1):
            copy.start()

    @pl.loop(1, spans)
    def _(step):
        @pl.when(me + step < spans)
        def _():
            for copy in listed(me, me + step):
                copy.start()

    for copy in keep:
        copy.wait()

    @pl.when(me > 0)
    def _():
        for copy in previous(me):
            copy.wait_recv()

    @pl.loop(1, spans)
    def _(step):
        @pl.when(me >= step)
        def _():
            for copy in listed(me - step, me):
                copy.wait_recv()

    offset = lax.broadcasted_iota(jnp.int32, (BLK, BLK), 1) - lax.broadcasted_iota(jnp.int32, (BLK, BLK), 0)

    @pl.loop(0, own)
    def _(b):
        for head in range(heads):
            columns = pl.ds(head * HEAD_DIM, HEAD_DIM)
            query = q[b, :, columns]
            top = jnp.full((BLK, BLK), -1e30, jnp.float32)
            for n in range(slots):
                keys = kpool[slot[b * slots + n], :, columns]
                part = lax.dot_general(query, keys, (((1,), (1,)), ((), ())), preferred_element_type=jnp.float32)
                part = jnp.where(offset <= reach[b * slots + n], part * HEAD_DIM**-0.5, -1e30)
                scores[n] = part
                top = jnp.maximum(top, part)
            top = jnp.max(top, axis=1, keepdims=True)
            total = jnp.zeros((BLK, BLK), jnp.float32)
            blended = jnp.zeros((BLK, HEAD_DIM), jnp.float32)
            for n in range(slots):
                weights = jnp.exp(scores[n] - top)
                total += weights
                values = vpool[slot[b * slots + n], :, columns]
                blended += jnp.dot(weights.astype(jnp.bfloat16), values, preferred_element_type=jnp.float32)
            total = jnp.sum(total, axis=1, keepdims=True)
            out[b, :, columns] = (blended / total).astype(jnp.bfloat16)

    @pl.when(me < spans - 1)
    def _():
        for copy in previous(me + 1):
            copy.wait_send()

    @pl.loop(1, spans)
    def _(step):
        @pl.when(me + step < spans)
        def _():
            for copy in listed(me, me + step):
                copy.wait_send()


def exchange_and_attend(q, k, v, layout, spans):
    rows, width = q.shape
    slots = 2 + layout.shape[1]
    pick, slot, reach = block_tables(layout, spans)
    own = rows // BLK
    pool = own + CAP * spans + 1
    q, k, v = (each.reshape(own, BLK, width) for each in (q, k, v))
    smem = pl.BlockSpec(memory_space=pltpu.SMEM)
    vmem = pl.BlockSpec(memory_space=pltpu.VMEM)
    return pl.pallas_call(
        functools.partial(attend_kernel, spans, slots),
        out_shape=jax.ShapeDtypeStruct((own, BLK, width), jnp.bfloat16),
        in_specs=[smem] * 3 + [vmem] * 3,
        out_specs=vmem,
        scratch_shapes=[
            pltpu.VMEM((pool, BLK, width), jnp.bfloat16),
            pltpu.VMEM((pool, BLK, width), jnp.bfloat16),
            pltpu.VMEM((spans * CAP, BLK, width), jnp.bfloat16),
            pltpu.VMEM((spans * CAP, BLK, width), jnp.bfloat16),
            pltpu.VMEM((slots, BLK, BLK), jnp.float32),
            pltpu.SemaphoreType.DMA((2,)),
            pltpu.SemaphoreType.DMA((spans + 1, 2)),
            pltpu.SemaphoreType.DMA((spans + 1, 2)),
        ],
        compiler_params=pltpu.CompilerParams(
            collective_id=0, has_side_effects=True, vmem_limit_bytes=48 * 2**20
        ),
    )(pick, slot, reach, q, k, v).reshape(rows, width)


def shards(spans, tokens, norm_gain, qkv_weight, out_weight, layout):
    normed = normalize(tokens, norm_gain)
    gathered = lax.all_gather(normed, "fsdp", axis=0, tiled=True)
    projected = jnp.einsum(
        "td,cdi->cti",
        gathered,
        lax.all_gather(qkv_weight, "ctx", axis=1, tiled=True),
        preferred_element_type=jnp.float32,
    ).astype(jnp.bfloat16)
    attended = exchange_and_attend(projected[0], projected[1], projected[2], layout, spans)
    projection = lax.all_gather(out_weight, "ctx", axis=1, tiled=True)
    return lax.psum_scatter(
        jnp.dot(attended, projection, preferred_element_type=jnp.float32).astype(jnp.bfloat16),
        "fsdp",
        scatter_dimension=0,
        tiled=True,
    )


def solution(mesh):
    placed = (P(("ctx", "fsdp"), None), P(), P(None, "ctx", "fsdp"), P("fsdp", "ctx"), P())
    return jax.shard_map(
        functools.partial(shards, mesh.shape["ctx"]),
        mesh=mesh, in_specs=placed, out_specs=P(("ctx", "fsdp"), None), check_vma=False,
    )
```

time: 464 us -> 294 us (0.63)
  waiting for transfers between devices: 309 us -> 173 us
  Pallas kernels: 0 us -> 82.2 us
  local copies, waits for them, and re-layouts: 80.5 us -> 2.04 us
  matrix products: 39.6 us -> 18.1 us
  other arithmetic: 19.8 us -> 4.21 us
    all_gather x2 -> x0, waiting for transfers between devices: 140 us -> none  [the longest x1 72.4 us: shards(): lax.all_gather(key_rows, 'ctx', axis=0, tiled=True)]
    pallas_call x0 -> x1, Pallas kernels: none -> 82.2 us  [exchange_and_attend(): pl.pallas_call(functools.partial(attend_kernel, spans, slots), out_shape=...]
    reshape x6 -> x3, local copies, waits for them, and re-layouts: 38.1 us -> 0.25 us  [the longest x1 0.09 us: block_tables(): pick = jnp.stack([lowest, highest], axis=1).reshape(-1)]
    gather x4 -> x0, local copies, waits for them, and re-layouts: 35.6 us -> none  [the longest x2 17.9 us: attend(): pool_values[group_index]]
    dot_general x2 -> x0, matrix products: 18.8 us -> none  [attend(): jnp.einsum('bhqnk,bnkhd->bqhd', weights, value_blocks, preferred_element_...]
    all_gather x1, waiting for transfers between devices: 0.02 us -> 7.93 us  [shards(): projection = lax.all_gather(out_weight, 'ctx', axis=1, tiled=True)]
    and x2 -> x0, other arithmetic: 7 us -> none  [attend(): (key_pos[:, None, :, :] <= query_pos[:, :, None, None]) & (key_pos[:, Non...]
    reduce_sum x2 -> x0, other arithmetic: 5.04 us -> none  [attend(): denominator = jnp.sum(weights, axis=(3, 4), keepdims=True)]
  transfers between devices with their start and end apart: 6 -> 4, of which waited for: 5 -> 4; matrix products, arithmetic and copies ran while one was open for 25% -> 6% of each run, Pallas kernels for 0% -> 28%
where the time goes in v1:
time: 294 us; the launch traced here: 293 us
  waiting for transfers between devices  173 us (59%)
  Pallas kernels  82.2 us (28%)
  matrix products  18.1 us (6%)
  between operations  13.2 us (4%)
  other arithmetic  4.21 us (1%)
    pallas_call x1, Pallas kernels, exchange_and_attend(): pl.pallas_call(functools.partial(attend_kernel, spans, slots), out_shape=...  82.2 us
    all_gather x1, waiting for transfers between devices, shards(): lax.all_gather(qkv_weight, 'ctx', axis=1, tiled=True)  56.5 us
    reduce_scatter x1, waiting for transfers between devices, shards(): lax.psum_scatter(jnp.dot(attended, projection, preferred_element_type=jnp...  54.3 us
    all_gather x1, waiting for transfers between devices, shards(): gathered = lax.all_gather(normed, 'fsdp', axis=0, tiled=True)  53.2 us
    dot_general x1, matrix products, shards(): jnp.einsum('td,cdi->cti', gathered, lax.all_gather(qkv_weight, 'ctx', axi...  10.9 us
    all_gather x1, waiting for transfers between devices, shards(): projection = lax.all_gather(out_weight, 'ctx', axis=1, tiled=True)  7.93 us
    dot_general x1, matrix products, shards(): jnp.dot(attended, projection, preferred_element_type=jnp.float32)  7.16 us
  transfers between devices with their start and end apart: 4, of which 4 were waited for; matrix products, arithmetic and copies ran while one was open for 6% of the time, Pallas kernels for 28%

profile of v1, /device:TPU:30, one launch (start us, length us, event | category | flops | bytes accessed | tf_op | source)
XLA Modules:
  0.0 293.3 jit_solution(13990691484026531745)
XLA Ops:
  6.5 0.0 copy-start
  6.5 0.0 all-gather.6.cloned.1.call-start
  6.5 0.7 all-gather.6.cloned.1.call-update
  7.3 0.0 copy-start.1
  7.3 0.0 all-gather.4.cloned.1.call-start
  7.3 1.5 fusion.2
  8.8 0.0 copy-done
  8.8 2.0 fusion.4
  10.9 0.0 all-gather.4.cloned.1.call-update
  10.9 0.0 all-gather.8.cloned.1.call-start
  10.9 0.7 all-gather.8.cloned.1.call-update
  11.6 0.0 reduce-scatter.2.cloned.1.call-start
  11.7 0.0 copy-done.1
  11.7 0.1 copy.10
  11.8 0.1 reshape.92
  11.9 0.5 broadcast.235
  12.4 0.6 fusion.18
  13.0 0.2 select_reduce_fusion
  13.2 0.1 reduce_min.31
  13.3 0.1 squeeze.6
  13.4 0.1 broadcast_subtract_fusion
  13.5 0.1 pad_add_fusion
  13.5 0.1 mul.44.reach
  13.6 0.1 reshape.93.slot
  13.7 0.1 reduce_min.28
  13.8 0.1 reduce_max.14
  13.9 0.1 reduce_min.29
  14.0 0.1 reduce_max.18
  14.2 0.1 copy.9
  14.2 0.1 reshape.91.pick
  14.3 56.5 %all-gather.6.cloned.1.call-done = bf16[3,4096,256]{2,1,0:T(8,128)(2,1)} async-done(((bf16[3,256,256]{2,1,0:T(8,128)(2,1)}), bf16[3,4096,256]{2,1,0:T(8,128)(2,1)}) %all-gather.6.cloned.1.call-update) | async-done | bytes 6291472 | tf_op jit(solution)/shard_map/all_gather | solution.py:197
  70.8 53.2 %all-gather.4.cloned.1.call-done = bf16[1024,4096]{1,0:T(8,128)(2,1)} async-done(((bf16[128,4096]{1,0:T(8,128)(2,1)}), bf16[1024,4096]{1,0:T(8,128)(2,1)}) %all-gather.4.cloned.1.call-update) | async-done | bytes 8388624 | tf_op jit(solution)/shard_map/all_gather | solution.py:193
  124.1 10.9 %fusion.8 = bf16[3,1024,256]{2,1,0:T(8,128)(2,1)S(1)} fusion(bf16[3,4096,256]{2,1,0:T(8,128)(2,1)} %all-gather.6.cloned.1.call-done, bf16[1024,4096]{1,0:T(8,128)(2,1)} %all-gather.4.cloned.1.call-done), kind=kOutput, calls=%fused_computation.9 | convolution fusion | flops 6443237376 | bytes 16252928 | tf_op jit(solution)/shard_map/td,cdi->cti/dot_general | solution.py:194
  135.0 0.1 fusion.19
  135.1 82.2 %shard_map.55 = bf16[8,128,256]{2,1,0:T(8,128)(2,1)S(1)} custom-call(s32[32]{0:T(128)S(1)} %reshape.91.pick, s32[144]{0:T(256)S(1)} %reshape.93.slot, s32[144]{0:T(256)S(1)} %mul.44.reach, bf16[8,128,256]{2,1,0:T(8,128)(2,1)S(1)} %bitcast.32, bf16[8,128,256]{2,1,0:T(8,128)(2,1)S(1)} %bitcast.31, bf16[8,128,256]{2,1,0:T(8,128)(2,1)S(1)} %bitcast.30), custom_call_target="tpu_custom_call" | custom-call | tf_op jit(solution)/shard_map/pallas_call | solution.py:170
  217.3 7.9 %all-gather.8.cloned.1.call-done = bf16[256,4096]{1,0:T(8,128)(2,1)} async-done(((bf16[256,256]{1,0:T(8,128)(2,1)}), bf16[256,4096]{1,0:T(8,128)(2,1)}) %all-gather.8.cloned.1.call-update) | async-done | bytes 2097168 | tf_op jit(solution)/shard_map/all_gather | solution.py:201
  225.2 7.2 %convolution_convert_fusion = bf16[1024,4096]{1,0:T(8,128)(2,1)} fusion(bf16[1024,256]{1,0:T(8,128)(2,1)S(1)} %bitcast.33, bf16[256,4096]{1,0:T(8,128)(2,1)} %all-gather.8.cloned.1.call-done), kind=kOutput, calls=%fused_computation.2 | convolution fusion | flops 2151677952 | bytes 11010048 | tf_op jit(solution)/shard_map/dot_general | solution.py:203
  232.4 0.0 reduce-scatter.2.cloned.1.call-update
  232.4 54.3 %reduce-scatter.2.cloned.1.call-done = bf16[128,4096]{1,0:T(8,128)(2,1)} async-done(((bf16[1024,4096]{1,0:T(8,128)(2,1)}), bf16[128,4096]{1,0:T(8,128)(2,1)}) %reduce-scatter.2.cloned.1.call-update) | async-done | bytes 1048592 | tf_op jit(solution)/shard_map/reduce_scatter | solution.py:202
  (10 shorter events, 0.1 us)
Async XLA Ops:
  6.5 2.3 copy-start
  6.5 64.3 %all-gather.6.cloned.1.call-start = ((), (), s32[]{:S(2)}) async-start(), calls=%async_computation.2 | async-start | bytes 6684672 | tf_op jit(solution)/shard_map/all_gather | solution.py:197
  7.3 4.4 %copy-start.1 = (s32[128,16]{0,1:T(8,128)S(1)}, s32[128,16]{0,1:T(8,128)}, u32[]{:S(2)}) copy-start(s32[128,16]{0,1:T(8,128)} %param.9) | copy-start | bytes 24580
  7.3 116.8 %all-gather.4.cloned.1.call-start = ((), (), s32[]{:S(2)}) async-start(), calls=%async_computation.1 | async-start | bytes 9437184 | tf_op jit(solution)/shard_map/all_gather | solution.py:193
  10.9 214.3 %all-gather.8.cloned.1.call-start = ((), (), s32[]{:S(2)}) async-start(), calls=%async_computation.3 | async-start | bytes 2228224 | tf_op jit(solution)/shard_map/all_gather | solution.py:201
  11.6 275.1 %reduce-scatter.2.cloned.1.call-start = ((), (), s32[]{:S(2)}) async-start(), calls=%async_computation.4 | async-start | bytes 9437184 | tf_op jit(solution)/shard_map/reduce_scatter | solution.py:202
Sparse Core Ops, SparseCore 0:
  9.5 61.2 all-gather.5
  72.6 51.4 all-gather.3
  126.2 98.9 all-gather.7
  232.5 54.1 reduce-scatter.1

commit v2 on v1

--- a/solution.py
+++ b/solution.py
@@ -1,4 +1,5 @@
 import functools
+import math
 
 import jax
 import jax.numpy as jnp
@@ -12,12 +13,6 @@
 EPSILON = 1e-05
 CAP = 2
 MESH = pl.DeviceIdType.MESH
-
-
-def normalize(tokens, norm_gain):
-    features = tokens.astype(jnp.float32)
-    mean_square = jnp.mean(features * features, axis=-1, keepdims=True)
-    return (features * lax.rsqrt(mean_square + EPSILON) * norm_gain).astype(jnp.bfloat16)
 
 
 def block_tables(layout, spans):
@@ -188,28 +183,235 @@
     )(pick, slot, reach, q, k, v).reshape(rows, width)
 
 
-def shards(spans, tokens, norm_gain, qkv_weight, out_weight, layout):
-    normed = normalize(tokens, norm_gain)
-    gathered = lax.all_gather(normed, "fsdp", axis=0, tiled=True)
-    projected = jnp.einsum(
-        "td,cdi->cti",
-        gathered,
-        lax.all_gather(qkv_weight, "ctx", axis=1, tiled=True),
-        preferred_element_type=jnp.float32,
+def gather_kernel(side, eps, tokens, gain, weights, projected, projection, rows_all, normed, held, send_t, recv_t, send_w, recv_w, own_sem):
+    ctx, lane = lax.axis_index("ctx"), lax.axis_index("fsdp")
+    x, y = ctx // side, lax.rem(ctx, side)
+    z, core = lane // 2, lax.rem(lane, 2)
+    part, width = tokens.shape
+    depth = weights.shape[1]
+    half, quarter = part // 2, depth // 4
+
+    def shift(at, by):
+        return lax.rem(at + by + side, side)
+
+    def along(axis, by):
+        if axis == "x":
+            return (shift(x, by) * side + y, lane)
+        if axis == "y":
+            return (x * side + shift(y, by), lane)
+        if axis == "z":
+            return (ctx, shift(z, by) * 2 + core)
+        return (ctx, z * 2 + 1 - core)
+
+    barrier = pltpu.get_barrier_semaphore()
+    peers = [along(axis, by) for axis in "xyz" for by in (1, -1)] + [along("core", 1)]
+    for peer in peers:
+        pl.semaphore_signal(barrier, inc=1, device_id=peer, device_id_type=MESH)
+
+    sent = []
+
+    def send_tokens(owner, h, peer, own=False):
+        there = rows_all.at[pl.ds(pl.multiple_of(owner * part + h * half, half), half)]
+        here = tokens.at[pl.ds(h * half, half)] if own else there
+        copy = pltpu.make_async_remote_copy(
+            here, there, send_t.at[len([c for c in sent if c[0] == "t"])], recv_t.at[owner, h], device_id=peer, device_id_type=MESH
+        )
+        copy.start()
+        sent.append(("t", copy))
+
+    def wait_tokens(owner, h):
+        there = rows_all.at[pl.ds(pl.multiple_of(owner * part + h * half, half), half)]
+        pltpu.make_async_remote_copy(
+            there, there, send_t.at[0], recv_t.at[owner, h], device_id=along("core", 1), device_id_type=MESH
+        ).wait_recv()
+
+    def piece_of(owner, p):
+        return held.at[:, pl.ds(pl.multiple_of(owner * depth + p * quarter, quarter), quarter)]
+
+    def send_weights(owner, p, peer, own=False):
+        there = piece_of(owner, p)
+        here = weights.at[:, pl.ds(p * quarter, quarter)] if own else there
+        copy = pltpu.make_async_remote_copy(
+            here, there, send_w.at[len([c for c in sent if c[0] == "w"])], recv_w.at[owner, p], device_id=peer, device_id_type=MESH
+        )
+        copy.start()
+        sent.append(("w", copy))
+
+    def wait_weights(owner, p):
+        pltpu.make_async_remote_copy(
+            piece_of(owner, p), piece_of(owner, p), send_w.at[0], recv_w.at[owner, p], device_id=along("core", 1), device_id_type=MESH
+        ).wait_recv()
+
+    def normalize_rows(owner):
+        @pl.loop(0, part // 16)
+        def _(n):
+            at = pl.ds(pl.multiple_of(owner * part + n * 16, 16), 16)
+            features = rows_all[at, :].astype(jnp.float32)
+            mean_square = jnp.mean(features * features, axis=-1, keepdims=True)
+            normed[at, :] = (features * lax.rsqrt(mean_square + eps) * gain[...]).astype(jnp.bfloat16)
+
+    keep = [
+        pltpu.make_async_copy(tokens, rows_all.at[pl.ds(pl.multiple_of(lane * part, part), part)], own_sem.at[0]),
+        pltpu.make_async_copy(weights, held.at[:, pl.ds(pl.multiple_of(ctx * depth, depth), depth)], own_sem.at[1]),
+    ]
+    for copy in keep:
+        copy.start()
+    pl.semaphore_wait(barrier, len(peers))
+
+    routes = (("x", "y", 0), ("y", "x", 2))
+
+    def owner_at(axis, by, other=0):
+        if axis == "x":
+            return shift(x, by) * side + shift(y, other)
+        return shift(x, other) * side + shift(y, by)
+
+    right, left, sibling = along("z", 1), along("z", -1), along("core", 1)
+    lane_at = lambda by, flip=0: shift(z, by) * 2 + (1 - core if flip else core)
+    send_tokens(lane, 0, right, own=True)
+    send_tokens(lane, 1, left, own=True)
+    for first, second, p in routes:
+        send_weights(ctx, p, along(first, 1), own=True)
+        send_weights(ctx, p + 1, along(first, -1), own=True)
+        send_weights(ctx, p + 1, along(first, 1), own=True)
+        send_weights(ctx, p, along(first, -1), own=True)
+    send_tokens(lane, 1, right, own=True)
+    send_tokens(lane, 0, left, own=True)
+    for h in range(2):
+        send_tokens(lane, h, sibling, own=True)
+    for first, second, p in routes:
+        send_weights(ctx, p, along(second, 1), own=True)
+        send_weights(ctx, p + 1, along(second, -1), own=True)
+        send_weights(ctx, p + 1, along(second, 1), own=True)
+        send_weights(ctx, p, along(second, -1), own=True)
+    for copy in keep:
+        copy.wait()
+    normalize_rows(lane)
+
+    def spread(owner, p, axis):
+        send_weights(owner, p, along(axis, 1))
+        send_weights(owner, p, along(axis, -1))
+
+    for first, second, p in routes:
+        wait_weights(owner_at(first, -1), p)
+        send_weights(owner_at(first, -1), p, along(first, 1))
+        wait_weights(owner_at(first, 1), p + 1)
+        send_weights(owner_at(first, 1), p + 1, along(first, -1))
+    for first, second, p in routes:
+        spread(owner_at(first, -1), p, second)
+        spread(owner_at(first, 1), p + 1, second)
+    for first, second, p in routes:
+        wait_weights(owner_at(first, -1), p + 1)
+        spread(owner_at(first, -1), p + 1, second)
+        wait_weights(owner_at(first, 1), p)
+        spread(owner_at(first, 1), p, second)
+
+    def relay(by):
+        for first, second, p in routes:
+            owner = owner_at(first, by, -1)
+            wait_weights(owner, p)
+            send_weights(owner, p, along(second, 1))
+            owner = owner_at(first, by, 1)
+            wait_weights(owner, p + 1)
+            send_weights(owner, p + 1, along(second, -1))
+
+    for first, second, p in routes:
+        for q in (p, p + 1):
+            wait_weights(owner_at(first, 2), q)
+            spread(owner_at(first, 2), q, second)
+    relay(0)
+    wait_tokens(lane_at(-1), 0)
+    send_tokens(lane_at(-1), 0, right)
+    send_tokens(lane_at(-1), 0, sibling)
+    wait_tokens(lane_at(1), 1)
+    send_tokens(lane_at(1), 1, left)
+    send_tokens(lane_at(1), 1, sibling)
+    relay(-1)
+    relay(1)
+    for h in range(2):
+        wait_tokens(lane_at(0, 1), h)
+    normalize_rows(lane_at(0, 1))
+    wait_tokens(lane_at(-1), 1)
+    send_tokens(lane_at(-1), 1, sibling)
+    wait_tokens(lane_at(1), 0)
+    send_tokens(lane_at(1), 0, sibling)
+    normalize_rows(lane_at(-1))
+    normalize_rows(lane_at(1))
+    relay(2)
+    for by in (-1, 1):
+        for h in range(2):
+            wait_tokens(lane_at(by, 1), h)
+        normalize_rows(lane_at(by, 1))
+    for h in range(2):
+        wait_tokens(lane_at(2), h)
+        send_tokens(lane_at(2), h, sibling)
+    normalize_rows(lane_at(2))
+    for first, second, p in routes:
+        for by in (0, -1, 1, 2):
+            wait_weights(owner_at(first, by, -1), p + 1)
+            wait_weights(owner_at(first, by, 1), p)
+            wait_weights(owner_at(first, by, 2), p)
+            wait_weights(owner_at(first, by, 2), p + 1)
+    for h in range(2):
+        wait_tokens(lane_at(2, 1), h)
+    normalize_rows(lane_at(2, 1))
+
+    tile = 256
+    steps = normed.shape[0] // tile
+    give = pltpu.make_async_copy(held.at[3], projection, own_sem.at[0])
+    give.start()
+
+    @pl.loop(0, 3 * steps)
+    def _(n):
+        which, at = n // steps, pl.ds(pl.multiple_of(lax.rem(n, steps) * tile, tile), tile)
+        projected[which, at, :] = jnp.dot(normed[at, :], held[which], preferred_element_type=jnp.float32).astype(jnp.bfloat16)
+
+    give.wait()
+    for _, copy in sent:
+        copy.wait_send()
+
+
+def gather_and_project(tokens, norm_gain, qkv_weight, out_weight, side, lanes):
+    part, width = tokens.shape
+    columns = qkv_weight.shape[2]
+    weights = jnp.concatenate([qkv_weight, out_weight[None]], axis=0)
+    vmem = pl.BlockSpec(memory_space=pltpu.VMEM)
+    return pl.pallas_call(
+        functools.partial(gather_kernel, side, EPSILON),
+        out_shape=[
+            jax.ShapeDtypeStruct((3, lanes * part, columns), jnp.bfloat16),
+            jax.ShapeDtypeStruct((width, columns), jnp.bfloat16),
+        ],
+        in_specs=[vmem] * 3,
+        out_specs=[vmem] * 2,
+        scratch_shapes=[
+            pltpu.VMEM((lanes * part, width), jnp.bfloat16),
+            pltpu.VMEM((lanes * part, width), jnp.bfloat16),
+            pltpu.VMEM((4, width, columns), jnp.bfloat16),
+            pltpu.SemaphoreType.DMA((14,)),
+            pltpu.SemaphoreType.DMA((lanes, 2)),
+            pltpu.SemaphoreType.DMA((60,)),
+            pltpu.SemaphoreType.DMA((side * side, 4)),
+            pltpu.SemaphoreType.DMA((2,)),
+        ],
+        compiler_params=pltpu.CompilerParams(
+            collective_id=1, has_side_effects=True, vmem_limit_bytes=60 * 2**20
+        ),
+    )(tokens, norm_gain[None, :], weights)
+
+
+def shards(spans, lanes, tokens, norm_gain, qkv_weight, out_weight, layout):
+    side = math.isqrt(spans)
+    projected, projection = gather_and_project(tokens, norm_gain, qkv_weight, out_weight, side, lanes)
+    attended = exchange_and_attend(projected[0], projected[1], projected[2], layout, spans)
+    product = jnp.einsum(
+        "tk,jkd->tjd", attended, projection.reshape(spans, -1, projection.shape[1]), preferred_element_type=jnp.float32
     ).astype(jnp.bfloat16)
-    attended = exchange_and_attend(projected[0], projected[1], projected[2], layout, spans)
-    projection = lax.all_gather(out_weight, "ctx", axis=1, tiled=True)
-    return lax.psum_scatter(
-        jnp.dot(attended, projection, preferred_element_type=jnp.float32).astype(jnp.bfloat16),
-        "fsdp",
-        scatter_dimension=0,
-        tiled=True,
-    )
+    return lax.psum_scatter(product.reshape(attended.shape[0], -1), "fsdp", scatter_dimension=0, tiled=True)
 
 
 def solution(mesh):
     placed = (P(("ctx", "fsdp"), None), P(), P(None, "ctx", "fsdp"), P("fsdp", "ctx"), P())
     return jax.shard_map(
-        functools.partial(shards, mesh.shape["ctx"]),
+        functools.partial(shards, mesh.shape["ctx"], mesh.shape["fsdp"]),
         mesh=mesh, in_specs=placed, out_specs=P(("ctx", "fsdp"), None), check_vma=False,
     )

time: 294 us -> 233 us (0.79)
  waiting for transfers between devices: 173 us -> 51.7 us
  Pallas kernels: 82.2 us -> 142 us
  local copies, waits for them, and re-layouts: 2.04 us -> 15.8 us
  matrix products: 18.1 us -> 5.61 us
    all_gather x3 -> x0, waiting for transfers between devices: 118 us -> none  [the longest x1 56.5 us: shards(): lax.all_gather(qkv_weight, 'ctx', axis=1, tiled=True)]
    pallas_call x0 -> x1, Pallas kernels: none -> 62 us  [gather_and_project(): pl.pallas_call(functools.partial(gather_kernel, side, EPSILON), out_shape...]
    dot_general x2 -> x1, matrix products: 18.1 us -> 5.61 us  [shards(): jnp.einsum('tk,jkd->tjd', attended, projection.reshape(spans, -1, project...]
    reshape x0 -> x1, local copies, waits for them, and re-layouts: none -> 11.5 us  [shards(): product.reshape(attended.shape[0], -1)]
  transfers between devices with their start and end apart: 4 -> 1, of which waited for: 4 -> 1; matrix products, arithmetic and copies ran while one was open for 6% -> 0% of each run, Pallas kernels for 28% -> 0%
where the time goes in v2:
time: 233 us; the launch traced here: 232 us
  Pallas kernels  142 us (61%)
  waiting for transfers between devices  51.7 us (22%)
  local copies, waits for them, and re-layouts  15.8 us (7%)
  between operations  13.5 us (6%)
  matrix products  5.61 us (2%)
  other arithmetic  3.28 us (1%)
    pallas_call x1, Pallas kernels, exchange_and_attend(): pl.pallas_call(functools.partial(attend_kernel, spans, slots), out_shape=...  80.2 us
    pallas_call x1, Pallas kernels, gather_and_project(): pl.pallas_call(functools.partial(gather_kernel, side, EPSILON), out_shape...  62 us
    reduce_scatter x1, waiting for transfers between devices, shards(): lax.psum_scatter(product.reshape(attended.shape[0], -1), 'fsdp', scatter_...  51.7 us
    reshape x1, local copies, waits for them, and re-layouts, shards(): product.reshape(attended.shape[0], -1)  11.5 us
    dot_general x1, matrix products, shards(): jnp.einsum('tk,jkd->tjd', attended, projection.reshape(spans, -1, project...  5.61 us
  transfers between devices with their start and end apart: 1, of which 1 were waited for; matrix products, arithmetic and copies ran while one was open for 0% of the time, Pallas kernels for 0%

profile of v2, /device:TPU:30, one launch (start us, length us, event | category | flops | bytes accessed | tf_op | source)
XLA Modules:
  0.0 232.1 jit_solution(14627181243196491646)
XLA Ops:
  6.5 0.0 reduce-scatter.2.cloned.1.call-start
  6.5 0.7 select_reduce_fusion.2
  7.3 0.8 copy.14
  8.1 0.1 reshape.89
  8.2 0.5 broadcast.223
  8.7 0.7 fusion.7
  9.4 0.1 reduce_min.28
  9.5 0.1 reduce_max.14
  9.5 0.1 reduce_min.29
  9.7 0.1 reduce_max.18
  9.8 0.1 copy.13
  9.9 0.1 reshape.88.pick
  10.0 0.2 select_reduce_fusion
  10.2 0.1 reduce_min.31
  10.2 0.1 squeeze.6
  10.3 0.1 broadcast_subtract_fusion
  10.4 0.1 pad_add_fusion
  10.5 0.1 reshape.90.slot
  10.6 0.1 mul.25.reach
  10.7 1.9 pad_maximum_fusion.weights
  12.6 62.0 %shard_map.55 = (bf16[3,1024,256]{2,1,0:T(8,128)(2,1)}, bf16[4096,256]{1,0:T(8,128)(2,1)}) custom-call(bf16[128,4096]{1,0:T(8,128)(2,1)} %tokens.1, f32[1,4096]{1,0:T(1,128)} %bitcast.33, bf16[4,256,256]{2,1,0:T(8,128)(2,1)} %pad_maximum_fusion.weights), custom_call_target="tpu_custom_call" | custom-call | tf_op jit(solution)/shard_map/pallas_call | solution.py:378
  74.6 0.0 copy-start
  74.6 1.6 fusion.8
  76.2 80.2 %shard_map.56 = bf16[8,128,256]{2,1,0:T(8,128)(2,1)S(1)} custom-call(s32[32]{0:T(128)S(1)} %reshape.88.pick, s32[144]{0:T(256)S(1)} %reshape.90.slot, s32[144]{0:T(256)S(1)} %mul.25.reach, bf16[8,128,256]{2,1,0:T(8,128)(2,1)S(1)} %bitcast.29, bf16[8,128,256]{2,1,0:T(8,128)(2,1)S(1)} %bitcast.28, bf16[8,128,256]{2,1,0:T(8,128)(2,1)S(1)} %bitcast.27), custom_call_target="tpu_custom_call" | custom-call | tf_op jit(solution)/shard_map/pallas_call | solution.py:165
  156.4 0.0 copy-done
  156.4 5.6 %convolution_convert_fusion = bf16[1024,16,256]{0,2,1:T(8,128)(2,1)} fusion(bf16[1024,256,1]{1,0,2:T(8,128)(2,1)S(1)} %bitcast.26, bf16[16,256,256]{2,1,0:T(8,128)(2,1)S(1)} %bitcast.31), kind=kOutput, calls=%fused_computation | convolution fusion | flops 2151677952 | bytes 11010048 | tf_op jit(solution)/shard_map/tk,jkd->tjd/dot_general | solution.py:406
  162.0 11.5 %copy.16 = bf16[1024,4096]{1,0:T(8,128)(2,1)} copy(bf16[1024,4096]{0,1:T(8,128)(2,1)} %bitcast.30) | data formatting | bytes 16777216 | tf_op jit(solution)/shard_map/reshape | solution.py:409
  173.5 0.0 reduce-scatter.2.cloned.1.call-update
  173.5 51.7 %reduce-scatter.2.cloned.1.call-done = bf16[128,4096]{1,0:T(8,128)(2,1)} async-done(((bf16[1024,4096]{1,0:T(8,128)(2,1)}), bf16[128,4096]{1,0:T(8,128)(2,1)}) %reduce-scatter.2.cloned.1.call-update) | async-done | bytes 1048592 | tf_op jit(solution)/shard_map/reduce_scatter | solution.py:409
  (8 shorter events, 0.0 us)
Async XLA Ops:
  6.5 218.7 %reduce-scatter.2.cloned.1.call-start = ((), (), s32[]{:S(2)}) async-start(), calls=%async_computation.1 | async-start | bytes 9437184 | tf_op jit(solution)/shard_map/reduce_scatter | solution.py:409
  74.6 81.8 %copy-start = (bf16[4096,256]{1,0:T(8,128)(2,1)S(1)}, bf16[4096,256]{1,0:T(8,128)(2,1)}, u32[]{:S(2)}) copy-start(bf16[4096,256]{1,0:T(8,128)(2,1)} %get-tuple-element.8) | copy-start | bytes 6291460
Sparse Core Ops, SparseCore 0:
  173.7 51.5 reduce-scatter.1

commit v3 on v2

--- a/solution.py
+++ b/solution.py
@@ -42,9 +42,19 @@
 
 
 def attend_kernel(
-    spans, slots, pick, slot, reach, q, k, v, out, kpool, vpool, kstage, vstage, scores, own_sem, send_sem, recv_sem
+    spans, slots, pick, slot, reach, q, k, v, projection, out,
+    kpool, vpool, kstage, vstage, scores, attended, partial, crossed, packed, hop, final,
+    own_sem, send_sem, recv_sem, cross_sem, sum_send, sum_recv,
 ):
     me, lane = lax.axis_index("ctx"), lax.axis_index("fsdp")
+    z, core = lane // 2, lax.rem(lane, 2)
+    chips = 4
+    pieces = projection.shape[0]
+    wide = projection.shape[2]
+    half = pieces // 2
+    right = (me, lax.rem(z + 1, chips) * 2 + core)
+    left = (me, lax.rem(z + chips - 1, chips) * 2 + core)
+    sibling = (me, z * 2 + 1 - core)
     own = q.shape[0]
     heads = q.shape[2] // HEAD_DIM
     barrier = pltpu.get_barrier_semaphore()
@@ -53,6 +63,9 @@
     def _(step):
         peer = lax.rem(me + step, spans)
         pl.semaphore_signal(barrier, inc=1, device_id=(peer, lane), device_id_type=MESH)
+
+    for peer in (right, left, sibling):
+        pl.semaphore_signal(barrier, inc=1, device_id=peer, device_id_type=MESH)
 
     keep = [
         pltpu.make_async_copy(k, kpool.at[pl.ds(0, own)], own_sem.at[0]),
@@ -66,7 +79,7 @@
         kstage[n] = k[pick[n]]
         vstage[n] = v[pick[n]]
 
-    pl.semaphore_wait(barrier, spans - 1)
+    pl.semaphore_wait(barrier, spans + 2)
 
     def listed(src, dst):
         there = pl.ds(own + CAP * src, CAP)
@@ -117,8 +130,7 @@
 
     offset = lax.broadcasted_iota(jnp.int32, (BLK, BLK), 1) - lax.broadcasted_iota(jnp.int32, (BLK, BLK), 0)
 
-    @pl.loop(0, own)
-    def _(b):
+    def attend(b, at):
         for head in range(heads):
             columns = pl.ds(head * HEAD_DIM, HEAD_DIM)
             query = q[b, :, columns]
@@ -138,7 +150,87 @@
                 values = vpool[slot[b * slots + n], :, columns]
                 blended += jnp.dot(weights.astype(jnp.bfloat16), values, preferred_element_type=jnp.float32)
             total = jnp.sum(total, axis=1, keepdims=True)
-            out[b, :, columns] = (blended / total).astype(jnp.bfloat16)
+            attended[at, :, columns] = (blended / total).astype(jnp.bfloat16)
+
+    def cross(g):
+        return pltpu.make_async_remote_copy(
+            partial.at[g, 0], crossed.at[g], cross_sem.at[0, g], cross_sem.at[1, g], device_id=sibling, device_id_type=MESH
+        )
+
+    def travel(n, source, target, peer):
+        return pltpu.make_async_remote_copy(
+            source, target, sum_send.at[n], sum_recv.at[n], device_id=peer, device_id_type=MESH
+        )
+
+    first, second = pl.ds(0, half), pl.ds(half, half)
+    travels = [
+        travel(0, packed.at[0, first], hop.at[0], right),
+        travel(1, packed.at[0, second], hop.at[1], left),
+        travel(2, packed.at[1, second], final.at[0, second], right),
+        travel(3, packed.at[1, first], final.at[0, first], right),
+        travel(4, packed.at[2, first], final.at[1, first], left),
+        travel(5, packed.at[2, second], final.at[1, second], left),
+    ]
+
+    def add(g, low, more=None):
+        @pl.loop(0, half)
+        def _(n):
+            term = partial[g, 1, low + n].astype(jnp.float32) + crossed[g, low + n].astype(jnp.float32)
+            if more is not None:
+                term += hop[more, n].astype(jnp.float32)
+            packed[g, low + n] = term.astype(jnp.bfloat16)
+
+    for g, steps in enumerate((2, 1, -1, 0)):
+        chip = lax.rem(z + steps + chips, chips)
+
+        @pl.loop(0, 2)
+        def _(turn):
+            attend(chip * 2 + lax.rem(core + 1 + turn, 2), turn)
+
+            @pl.loop(0, pieces)
+            def _(n):
+                partial[g, turn, n] = jnp.dot(
+                    attended[turn], projection[n], preferred_element_type=jnp.float32
+                ).astype(jnp.bfloat16)
+
+            @pl.when(turn == 0)
+            def _():
+                cross(g).start()
+
+        cross(g).wait_recv()
+        if g == 0:
+            add(0, 0)
+            travels[0].start()
+            add(0, half)
+            travels[1].start()
+        elif g == 1:
+            add(1, half)
+            travels[2].start()
+            travels[0].wait_recv()
+            add(1, 0, 0)
+            travels[3].start()
+        elif g == 2:
+            add(2, 0)
+            travels[4].start()
+            travels[1].wait_recv()
+            add(2, half, 1)
+            travels[5].start()
+
+    for low, waits in ((half, (2, 5)), (0, (3, 4))):
+        for n in waits:
+            travels[n].wait_recv()
+
+        @pl.loop(0, half)
+        def _(n):
+            at = low + n
+            term = partial[3, 1, at].astype(jnp.float32) + crossed[3, at].astype(jnp.float32)
+            term += final[0, at].astype(jnp.float32) + final[1, at].astype(jnp.float32)
+            out[:, pl.ds(pl.multiple_of(at * wide, wide), wide)] = term.astype(jnp.bfloat16)
+
+    for g in range(chips):
+        cross(g).wait_send()
+    for copy in travels:
+        copy.wait_send()
 
     @pl.when(me < spans - 1)
     def _():
@@ -153,19 +245,21 @@
                 copy.wait_send()
 
 
-def exchange_and_attend(q, k, v, layout, spans):
+def attend_and_reduce(q, k, v, projection, layout, spans):
     rows, width = q.shape
     slots = 2 + layout.shape[1]
     pick, slot, reach = block_tables(layout, spans)
     own = rows // BLK
     pool = own + CAP * spans + 1
+    pieces, _, wide = projection.shape
+    whole = (pieces, BLK, wide)
     q, k, v = (each.reshape(own, BLK, width) for each in (q, k, v))
     smem = pl.BlockSpec(memory_space=pltpu.SMEM)
     vmem = pl.BlockSpec(memory_space=pltpu.VMEM)
     return pl.pallas_call(
         functools.partial(attend_kernel, spans, slots),
-        out_shape=jax.ShapeDtypeStruct((own, BLK, width), jnp.bfloat16),
-        in_specs=[smem] * 3 + [vmem] * 3,
+        out_shape=jax.ShapeDtypeStruct((BLK, pieces * wide), jnp.bfloat16),
+        in_specs=[smem] * 3 + [vmem] * 4,
         out_specs=vmem,
         scratch_shapes=[
             pltpu.VMEM((pool, BLK, width), jnp.bfloat16),
@@ -173,14 +267,23 @@
             pltpu.VMEM((spans * CAP, BLK, width), jnp.bfloat16),
             pltpu.VMEM((spans * CAP, BLK, width), jnp.bfloat16),
             pltpu.VMEM((slots, BLK, BLK), jnp.float32),
+            pltpu.VMEM((2, BLK, width), jnp.bfloat16),
+            pltpu.VMEM((4, 2, *whole), jnp.bfloat16),
+            pltpu.VMEM((4, *whole), jnp.bfloat16),
+            pltpu.VMEM((3, *whole), jnp.bfloat16),
+            pltpu.VMEM((2, pieces // 2, BLK, wide), jnp.bfloat16),
+            pltpu.VMEM((2, *whole), jnp.bfloat16),
             pltpu.SemaphoreType.DMA((2,)),
             pltpu.SemaphoreType.DMA((spans + 1, 2)),
             pltpu.SemaphoreType.DMA((spans + 1, 2)),
+            pltpu.SemaphoreType.DMA((2, 4)),
+            pltpu.SemaphoreType.DMA((6,)),
+            pltpu.SemaphoreType.DMA((6,)),
         ],
         compiler_params=pltpu.CompilerParams(
-            collective_id=0, has_side_effects=True, vmem_limit_bytes=48 * 2**20
+            collective_id=0, has_side_effects=True, vmem_limit_bytes=60 * 2**20
         ),
-    )(pick, slot, reach, q, k, v).reshape(rows, width)
+    )(pick, slot, reach, q, k, v, projection)
 
 
 def gather_kernel(side, eps, tokens, gain, weights, projected, projection, rows_all, normed, held, send_t, recv_t, send_w, recv_w, own_sem):
@@ -402,11 +505,8 @@
 def shards(spans, lanes, tokens, norm_gain, qkv_weight, out_weight, layout):
     side = math.isqrt(spans)
     projected, projection = gather_and_project(tokens, norm_gain, qkv_weight, out_weight, side, lanes)
-    attended = exchange_and_attend(projected[0], projected[1], projected[2], layout, spans)
-    product = jnp.einsum(
-        "tk,jkd->tjd", attended, projection.reshape(spans, -1, projection.shape[1]), preferred_element_type=jnp.float32
-    ).astype(jnp.bfloat16)
-    return lax.psum_scatter(product.reshape(attended.shape[0], -1), "fsdp", scatter_dimension=0, tiled=True)
+    projection = projection.reshape(spans, -1, projection.shape[1])
+    return attend_and_reduce(projected[0], projected[1], projected[2], projection, layout, spans)
 
 
 def solution(mesh):

time: 233 us -> 198 us (0.85)
  waiting for transfers between devices: 51.7 us -> 0 us
  Pallas kernels: 142 us -> 186 us
  between operations: 13.5 us -> 0.08 us
  local copies, waits for them, and re-layouts: 15.8 us -> 9.26 us
  matrix products: 5.61 us -> 0 us
    reduce_scatter x1 -> x0, waiting for transfers between devices: 51.7 us -> none  [shards(): lax.psum_scatter(product.reshape(attended.shape[0], -1), 'fsdp', scatter_...]
    pallas_call x1, Pallas kernels: 80.2 us -> 124 us  [attend_and_reduce(): pl.pallas_call(functools.partial(attend_kernel, spans, slots), out_shape=...]
    reshape x1 -> x0, local copies, waits for them, and re-layouts: 11.5 us -> none  [shards(): product.reshape(attended.shape[0], -1)]
    dot_general x1 -> x0, matrix products: 5.61 us -> none  [shards(): jnp.einsum('tk,jkd->tjd', attended, projection.reshape(spans, -1, project...]
  transfers between devices with their start and end apart: 1 -> 0, of which waited for: 1 -> 0; matrix products, arithmetic and copies ran while one was open for 0% -> 0% of each run, Pallas kernels for 0% -> 0%
where the time goes in v3:
time: 198 us
  Pallas kernels  186 us (94%)
  local copies, waits for them, and re-layouts  9.26 us (5%)
  other arithmetic  3.27 us (2%)
    pallas_call x1, Pallas kernels, attend_and_reduce(): pl.pallas_call(functools.partial(attend_kernel, spans, slots), out_shape=...  124 us
    pallas_call x1, Pallas kernels, gather_and_project(): pl.pallas_call(functools.partial(gather_kernel, side, EPSILON), out_shape...  62 us

profile of v3, /device:TPU:30, one launch (start us, length us, event | category | flops | bytes accessed | tf_op | source)
XLA Modules:
  0.0 198.1 jit_solution(11694808353350518071)
XLA Ops:
  0.0 0.7 select_reduce_fusion.2
  0.8 0.1 reduce_min.28
  0.8 0.1 reduce_min.29
  1.0 0.1 reduce_max.14
  1.1 0.1 reduce_max.18
  1.2 0.1 copy.9
  1.3 0.7 reshape.82.pick
  2.0 0.8 copy.10
  2.7 0.1 reshape.83
  2.8 0.5 broadcast.223
  3.3 0.7 fusion.7
  4.0 0.2 select_reduce_fusion
  4.2 0.1 reduce_min.31
  4.3 0.1 squeeze.6
  4.4 0.1 broadcast_subtract_fusion
  4.5 0.1 pad_add_fusion
  4.5 0.7 reshape.84.slot
  5.2 0.7 mul.25.reach
  5.9 1.9 pad_maximum_fusion.weights
  7.8 62.0 %shard_map.55 = (bf16[3,1024,256]{2,1,0:T(8,128)(2,1)}, bf16[4096,256]{1,0:T(8,128)(2,1)}) custom-call(bf16[128,4096]{1,0:T(8,128)(2,1)} %tokens.1, f32[1,4096]{1,0:T(1,128)} %bitcast.25, bf16[4,256,256]{2,1,0:T(8,128)(2,1)} %pad_maximum_fusion.weights), custom_call_target="tpu_custom_call" | custom-call | tf_op jit(solution)/shard_map/pallas_call | solution.py:481
  69.7 2.5 %fusion.8 = (bf16[1,1024,256]{2,1,0:T(8,128)(2,1)}, bf16[1,1024,256]{2,1,0:T(8,128)(2,1)}, bf16[1,1024,256]{2,1,0:T(8,128)(2,1)}) fusion(bf16[3,1024,256]{2,1,0:T(8,128)(2,1)} %get-tuple-element.7), kind=kLoop, calls=%fused_computation.44 | loop fusion | bytes 3145728 | tf_op jit(solution)/shard_map/slice | solution.py:509
  72.3 123.6 %shard_map.56 = bf16[128,4096]{1,0:T(8,128)(2,1)} custom-call(s32[32]{0:T(128)} %reshape.82.pick, s32[144]{0:T(256)} %reshape.84.slot, s32[144]{0:T(256)} %mul.25.reach, bf16[8,128,256]{2,1,0:T(8,128)(2,1)} %bitcast.23, bf16[8,128,256]{2,1,0:T(8,128)(2,1)} %bitcast.22, bf16[8,128,256]{2,1,0:T(8,128)(2,1)} %bitcast.21, bf16[16,256,256]{2,1,0:T(8,128)(2,1)} %bitcast.20), custom_call_target="tpu_custom_call" | custom-call | tf_op jit(solution)/shard_map/pallas_call | solution.py:259
  195.8 2.3 %copy.12 = bf16[128,4096]{1,0:T(8,128)(2,1)} copy(bf16[128,4096]{1,0:T(8,128)(2,1)} %shard_map.56) | data formatting | bytes 2097152
  (8 shorter events, 0.1 us)

commit v4 on v3

--- a/solution.py
+++ b/solution.py
@@ -42,11 +42,12 @@
 
 
 def attend_kernel(
-    spans, slots, pick, slot, reach, q, k, v, projection, out,
+    spans, slots, pick, slot, reach, projected, projection, out,
     kpool, vpool, kstage, vstage, scores, attended, partial, crossed, packed, hop, final,
     own_sem, send_sem, recv_sem, cross_sem, sum_send, sum_recv,
 ):
     me, lane = lax.axis_index("ctx"), lax.axis_index("fsdp")
+    q, k, v = (projected.at[which] for which in range(3))
     z, core = lane // 2, lax.rem(lane, 2)
     chips = 4
     pieces = projection.shape[0]
@@ -206,12 +207,12 @@
         elif g == 1:
             add(1, half)
             travels[2].start()
+        elif g == 2:
+            add(2, 0)
+            travels[4].start()
             travels[0].wait_recv()
             add(1, 0, 0)
             travels[3].start()
-        elif g == 2:
-            add(2, 0)
-            travels[4].start()
             travels[1].wait_recv()
             add(2, half, 1)
             travels[5].start()
@@ -245,21 +246,21 @@
                 copy.wait_send()
 
 
-def attend_and_reduce(q, k, v, projection, layout, spans):
-    rows, width = q.shape
+def attend_and_reduce(projected, projection, layout, spans):
+    _, rows, width = projected.shape
     slots = 2 + layout.shape[1]
     pick, slot, reach = block_tables(layout, spans)
     own = rows // BLK
     pool = own + CAP * spans + 1
     pieces, _, wide = projection.shape
     whole = (pieces, BLK, wide)
-    q, k, v = (each.reshape(own, BLK, width) for each in (q, k, v))
+    projected = projected.reshape(3, own, BLK, width)
     smem = pl.BlockSpec(memory_space=pltpu.SMEM)
     vmem = pl.BlockSpec(memory_space=pltpu.VMEM)
     return pl.pallas_call(
         functools.partial(attend_kernel, spans, slots),
         out_shape=jax.ShapeDtypeStruct((BLK, pieces * wide), jnp.bfloat16),
-        in_specs=[smem] * 3 + [vmem] * 4,
+        in_specs=[smem] * 3 + [vmem] * 2,
         out_specs=vmem,
         scratch_shapes=[
             pltpu.VMEM((pool, BLK, width), jnp.bfloat16),
@@ -283,7 +284,7 @@
         compiler_params=pltpu.CompilerParams(
             collective_id=0, has_side_effects=True, vmem_limit_bytes=60 * 2**20
         ),
-    )(pick, slot, reach, q, k, v, projection)
+    )(pick, slot, reach, projected, projection)
 
 
 def gather_kernel(side, eps, tokens, gain, weights, projected, projection, rows_all, normed, held, send_t, recv_t, send_w, recv_w, own_sem):
@@ -506,7 +507,7 @@
     side = math.isqrt(spans)
     projected, projection = gather_and_project(tokens, norm_gain, qkv_weight, out_weight, side, lanes)
     projection = projection.reshape(spans, -1, projection.shape[1])
-    return attend_and_reduce(projected[0], projected[1], projected[2], projection, layout, spans)
+    return attend_and_reduce(projected, projection, layout, spans)
 
 
 def solution(mesh):

time: 198 us -> 192 us (0.970)
  Pallas kernels: 186 us -> 181 us
  local copies, waits for them, and re-layouts: 9.26 us -> 6.73 us
    pallas_call x1, Pallas kernels: 124 us -> 119 us  [attend_and_reduce(): pl.pallas_call(functools.partial(attend_kernel, spans, slots), out_shape=...]
    slice x1 -> x0, local copies, waits for them, and re-layouts: 2.53 us -> none  [shards(): projected[2]]
where the time goes in v4:
time: 192 us; the launch traced here: 191 us
  Pallas kernels  181 us (94%)
  local copies, waits for them, and re-layouts  6.73 us (4%)
  other arithmetic  3.27 us (2%)
    pallas_call x1, Pallas kernels, attend_and_reduce(): pl.pallas_call(functools.partial(attend_kernel, spans, slots), out_shape=...  119 us
    pallas_call x1, Pallas kernels, gather_and_project(): pl.pallas_call(functools.partial(gather_kernel, side, EPSILON), out_shape...  62 us

profile of v4, /device:TPU:30, one launch (start us, length us, event | category | flops | bytes accessed | tf_op | source)
XLA Modules:
  0.0 191.4 jit_solution(6101731941190888232)
XLA Ops:
  0.0 0.7 select_reduce_fusion.2
  0.8 0.1 reduce_min.28
  0.8 0.1 reduce_min.29
  1.0 0.1 reduce_max.14
  1.1 0.1 reduce_max.18
  1.2 0.1 copy.9
  1.3 0.7 reshape.85.pick
  2.0 0.8 copy.10
  2.7 0.1 reshape.86
  2.8 0.5 broadcast.223
  3.3 0.7 fusion.7
  4.0 0.2 select_reduce_fusion
  4.2 0.1 reduce_min.31
  4.3 0.1 squeeze.6
  4.4 0.1 broadcast_subtract_fusion
  4.5 0.1 pad_add_fusion
  4.5 0.7 reshape.87.slot
  5.2 0.7 mul.25.reach
  5.9 1.9 pad_maximum_fusion.weights
  7.8 62.0 %shard_map.55 = (bf16[3,1024,256]{2,1,0:T(8,128)(2,1)}, bf16[4096,256]{1,0:T(8,128)(2,1)}) custom-call(bf16[128,4096]{1,0:T(8,128)(2,1)} %tokens.1, f32[1,4096]{1,0:T(1,128)} %bitcast.21, bf16[4,256,256]{2,1,0:T(8,128)(2,1)} %pad_maximum_fusion.weights), custom_call_target="tpu_custom_call" | custom-call | tf_op jit(solution)/shard_map/pallas_call | solution.py:482
  69.7 119.4 %shard_map.56 = bf16[128,4096]{1,0:T(8,128)(2,1)} custom-call(s32[32]{0:T(128)} %reshape.85.pick, s32[144]{0:T(256)} %reshape.87.slot, s32[144]{0:T(256)} %mul.25.reach, bf16[3,8,128,256]{3,2,1,0:T(8,128)(2,1)} %bitcast.19, bf16[16,256,256]{2,1,0:T(8,128)(2,1)} %bitcast.18), custom_call_target="tpu_custom_call" | custom-call | tf_op jit(solution)/shard_map/pallas_call | solution.py:260
  189.1 2.3 %copy.12 = bf16[128,4096]{1,0:T(8,128)(2,1)} copy(bf16[128,4096]{1,0:T(8,128)(2,1)} %shard_map.56) | data formatting | bytes 2097152
  (8 shorter events, 0.1 us)

commit v5 on v1

--- a/solution.py
+++ b/solution.py
@@ -1,4 +1,5 @@
 import functools
+import math
 
 import jax
 import jax.numpy as jnp
@@ -12,12 +13,6 @@
 EPSILON = 1e-05
 CAP = 2
 MESH = pl.DeviceIdType.MESH
-
-
-def normalize(tokens, norm_gain):
-    features = tokens.astype(jnp.float32)
-    mean_square = jnp.mean(features * features, axis=-1, keepdims=True)
-    return (features * lax.rsqrt(mean_square + EPSILON) * norm_gain).astype(jnp.bfloat16)
 
 
 def block_tables(layout, spans):
@@ -46,12 +41,194 @@
     return pick.astype(jnp.int32), slot.reshape(-1).astype(jnp.int32), reach.reshape(-1).astype(jnp.int32)
 
 
+def gather(side, eps, enter, tokens, gain, weights, rows_all, normed, held, send_t, recv_t, send_w, recv_w, own_sem):
+    ctx, lane = lax.axis_index("ctx"), lax.axis_index("fsdp")
+    x, y = ctx // side, lax.rem(ctx, side)
+    z, core = lane // 2, lax.rem(lane, 2)
+    part, width = tokens.shape
+    depth = weights.shape[1]
+    half, quarter = part // 2, depth // 4
+
+    def shift(at, by):
+        return lax.rem(at + by + side, side)
+
+    def along(axis, by):
+        if axis == "x":
+            return (shift(x, by) * side + y, lane)
+        if axis == "y":
+            return (x * side + shift(y, by), lane)
+        if axis == "z":
+            return (ctx, shift(z, by) * 2 + core)
+        return (ctx, z * 2 + 1 - core)
+
+    sent = []
+
+    def send_tokens(owner, h, peer, own=False):
+        there = rows_all.at[pl.ds(pl.multiple_of(owner * part + h * half, half), half)]
+        here = tokens.at[pl.ds(h * half, half)] if own else there
+        copy = pltpu.make_async_remote_copy(
+            here, there, send_t.at[len([c for c in sent if c[0] == "t"])], recv_t.at[owner, h], device_id=peer, device_id_type=MESH
+        )
+        copy.start()
+        sent.append(("t", copy))
+
+    def wait_tokens(owner, h):
+        there = rows_all.at[pl.ds(pl.multiple_of(owner * part + h * half, half), half)]
+        pltpu.make_async_remote_copy(
+            there, there, send_t.at[0], recv_t.at[owner, h], device_id=along("core", 1), device_id_type=MESH
+        ).wait_recv()
+
+    def piece_of(owner, p):
+        return held.at[:, pl.ds(pl.multiple_of(owner * depth + p * quarter, quarter), quarter)]
+
+    def send_weights(owner, p, peer, own=False):
+        there = piece_of(owner, p)
+        here = weights.at[:, pl.ds(p * quarter, quarter)] if own else there
+        copy = pltpu.make_async_remote_copy(
+            here, there, send_w.at[len([c for c in sent if c[0] == "w"])], recv_w.at[owner, p], device_id=peer, device_id_type=MESH
+        )
+        copy.start()
+        sent.append(("w", copy))
+
+    def wait_weights(owner, p):
+        pltpu.make_async_remote_copy(
+            piece_of(owner, p), piece_of(owner, p), send_w.at[0], recv_w.at[owner, p], device_id=along("core", 1), device_id_type=MESH
+        ).wait_recv()
+
+    def normalize_rows(owner):
+        @pl.loop(0, part // 16)
+        def _(n):
+            at = pl.ds(pl.multiple_of(owner * part + n * 16, 16), 16)
+            features = rows_all[at, :].astype(jnp.float32)
+            mean_square = jnp.mean(features * features, axis=-1, keepdims=True)
+            normed[at, :] = (features * lax.rsqrt(mean_square + eps) * gain[...]).astype(jnp.bfloat16)
+
+    keep = [
+        pltpu.make_async_copy(tokens, rows_all.at[pl.ds(pl.multiple_of(lane * part, part), part)], own_sem.at[0]),
+        pltpu.make_async_copy(weights, held.at[:, pl.ds(pl.multiple_of(ctx * depth, depth), depth)], own_sem.at[1]),
+    ]
+    for copy in keep:
+        copy.start()
+    enter()
+
+    routes = (("x", "y", 0), ("y", "x", 2))
+
+    def owner_at(axis, by, other=0):
+        if axis == "x":
+            return shift(x, by) * side + shift(y, other)
+        return shift(x, other) * side + shift(y, by)
+
+    right, left, sibling = along("z", 1), along("z", -1), along("core", 1)
+    lane_at = lambda by, flip=0: shift(z, by) * 2 + (1 - core if flip else core)
+    send_tokens(lane, 0, right, own=True)
+    send_tokens(lane, 1, left, own=True)
+    for first, second, p in routes:
+        send_weights(ctx, p, along(first, 1), own=True)
+        send_weights(ctx, p + 1, along(first, -1), own=True)
+        send_weights(ctx, p + 1, along(first, 1), own=True)
+        send_weights(ctx, p, along(first, -1), own=True)
+    send_tokens(lane, 1, right, own=True)
+    send_tokens(lane, 0, left, own=True)
+    for h in range(2):
+        send_tokens(lane, h, sibling, own=True)
+    for first, second, p in routes:
+        send_weights(ctx, p, along(second, 1), own=True)
+        send_weights(ctx, p + 1, along(second, -1), own=True)
+        send_weights(ctx, p + 1, along(second, 1), own=True)
+        send_weights(ctx, p, along(second, -1), own=True)
+    for copy in keep:
+        copy.wait()
+    normalize_rows(lane)
+
+    def spread(owner, p, axis):
+        send_weights(owner, p, along(axis, 1))
+        send_weights(owner, p, along(axis, -1))
+
+    for first, second, p in routes:
+        wait_weights(owner_at(first, -1), p)
+        send_weights(owner_at(first, -1), p, along(first, 1))
+        wait_weights(owner_at(first, 1), p + 1)
+        send_weights(owner_at(first, 1), p + 1, along(first, -1))
+    for first, second, p in routes:
+        spread(owner_at(first, -1), p, second)
+        spread(owner_at(first, 1), p + 1, second)
+    for first, second, p in routes:
+        wait_weights(owner_at(first, -1), p + 1)
+        spread(owner_at(first, -1), p + 1, second)
+        wait_weights(owner_at(first, 1), p)
+        spread(owner_at(first, 1), p, second)
+
+    def relay(by):
+        for first, second, p in routes:
+            owner = owner_at(first, by, -1)
+            wait_weights(owner, p)
+            send_weights(owner, p, along(second, 1))
+            owner = owner_at(first, by, 1)
+            wait_weights(owner, p + 1)
+            send_weights(owner, p + 1, along(second, -1))
+
+    for first, second, p in routes:
+        for q in (p, p + 1):
+            wait_weights(owner_at(first, 2), q)
+            spread(owner_at(first, 2), q, second)
+    relay(0)
+    wait_tokens(lane_at(-1), 0)
+    send_tokens(lane_at(-1), 0, right)
+    send_tokens(lane_at(-1), 0, sibling)
+    wait_tokens(lane_at(1), 1)
+    send_tokens(lane_at(1), 1, left)
+    send_tokens(lane_at(1), 1, sibling)
+    relay(-1)
+    relay(1)
+    for h in range(2):
+        wait_tokens(lane_at(0, 1), h)
+    normalize_rows(lane_at(0, 1))
+    wait_tokens(lane_at(-1), 1)
+    send_tokens(lane_at(-1), 1, sibling)
+    wait_tokens(lane_at(1), 0)
+    send_tokens(lane_at(1), 0, sibling)
+    normalize_rows(lane_at(-1))
+    normalize_rows(lane_at(1))
+    relay(2)
+    for by in (-1, 1):
+        for h in range(2):
+            wait_tokens(lane_at(by, 1), h)
+        normalize_rows(lane_at(by, 1))
+    for h in range(2):
+        wait_tokens(lane_at(2), h)
+        send_tokens(lane_at(2), h, sibling)
+    normalize_rows(lane_at(2))
+    for first, second, p in routes:
+        for by in (0, -1, 1, 2):
+            wait_weights(owner_at(first, by, -1), p + 1)
+            wait_weights(owner_at(first, by, 1), p)
+            wait_weights(owner_at(first, by, 2), p)
+            wait_weights(owner_at(first, by, 2), p + 1)
+    for h in range(2):
+        wait_tokens(lane_at(2, 1), h)
+    normalize_rows(lane_at(2, 1))
+
+    return [copy for _, copy in sent]
+
+
 def attend_kernel(
-    spans, slots, pick, slot, reach, q, k, v, out, kpool, vpool, kstage, vstage, scores, own_sem, send_sem, recv_sem
+    side, spans, slots, pick, slot, reach, tokens, gain, weights, out, rows_all, normed, held, projected,
+    kpool, vpool, kstage, vstage, scores, attended, partial, crossed, packed, hop, final,
+    send_t, recv_t, send_w, recv_w, own_sem, send_sem, recv_sem, cross_sem, sum_send, sum_recv,
 ):
     me, lane = lax.axis_index("ctx"), lax.axis_index("fsdp")
+    q, k, v = (projected.at[which] for which in range(3))
+    z, core = lane // 2, lax.rem(lane, 2)
+    chips = 4
+    pieces, wide = spans, held.shape[2]
+    projection = held.at[3]
+    half = pieces // 2
+    right = (me, lax.rem(z + 1, chips) * 2 + core)
+    left = (me, lax.rem(z + chips - 1, chips) * 2 + core)
+    sibling = (me, z * 2 + 1 - core)
     own = q.shape[0]
-    heads = q.shape[2] // HEAD_DIM
+    width = q.shape[2]
+    heads = width // HEAD_DIM
     barrier = pltpu.get_barrier_semaphore()
 
     @pl.loop(1, spans)
@@ -59,6 +236,24 @@
         peer = lax.rem(me + step, spans)
         pl.semaphore_signal(barrier, inc=1, device_id=(peer, lane), device_id_type=MESH)
 
+    for peer in (right, left, sibling):
+        pl.semaphore_signal(barrier, inc=1, device_id=peer, device_id_type=MESH)
+
+    sent = gather(
+        side, EPSILON, lambda: pl.semaphore_wait(barrier, spans + 2), tokens, gain, weights,
+        rows_all, normed, held, send_t, recv_t, send_w, recv_w, own_sem,
+    )
+    tile = 2 * BLK
+
+    def project(which):
+        @pl.loop(0, normed.shape[0] // tile)
+        def _(n):
+            rows = normed[pl.ds(pl.multiple_of(n * tile, tile), tile), :]
+            product = jnp.dot(rows, held[which], preferred_element_type=jnp.float32)
+            projected[which, pl.ds(2 * n, 2)] = product.astype(jnp.bfloat16).reshape(2, BLK, width)
+
+    project(1)
+    project(2)
     keep = [
         pltpu.make_async_copy(k, kpool.at[pl.ds(0, own)], own_sem.at[0]),
         pltpu.make_async_copy(v, vpool.at[pl.ds(0, own)], own_sem.at[1]),
@@ -70,8 +265,6 @@
     def _(n):
         kstage[n] = k[pick[n]]
         vstage[n] = v[pick[n]]
-
-    pl.semaphore_wait(barrier, spans - 1)
 
     def listed(src, dst):
         there = pl.ds(own + CAP * src, CAP)
@@ -105,6 +298,7 @@
             for copy in listed(me, me + step):
                 copy.start()
 
+    project(0)
     for copy in keep:
         copy.wait()
 
@@ -122,8 +316,7 @@
 
     offset = lax.broadcasted_iota(jnp.int32, (BLK, BLK), 1) - lax.broadcasted_iota(jnp.int32, (BLK, BLK), 0)
 
-    @pl.loop(0, own)
-    def _(b):
+    def attend(b, at):
         for head in range(heads):
             columns = pl.ds(head * HEAD_DIM, HEAD_DIM)
             query = q[b, :, columns]
@@ -143,7 +336,87 @@
                 values = vpool[slot[b * slots + n], :, columns]
                 blended += jnp.dot(weights.astype(jnp.bfloat16), values, preferred_element_type=jnp.float32)
             total = jnp.sum(total, axis=1, keepdims=True)
-            out[b, :, columns] = (blended / total).astype(jnp.bfloat16)
+            attended[at, :, columns] = (blended / total).astype(jnp.bfloat16)
+
+    def cross(g):
+        return pltpu.make_async_remote_copy(
+            partial.at[g, 0], crossed.at[g], cross_sem.at[0, g], cross_sem.at[1, g], device_id=sibling, device_id_type=MESH
+        )
+
+    def travel(n, source, target, peer):
+        return pltpu.make_async_remote_copy(
+            source, target, sum_send.at[n], sum_recv.at[n], device_id=peer, device_id_type=MESH
+        )
+
+    first, second = pl.ds(0, half), pl.ds(half, half)
+    travels = [
+        travel(0, packed.at[0, first], hop.at[0], right),
+        travel(1, packed.at[0, second], hop.at[1], left),
+        travel(2, packed.at[1, second], final.at[0, second], right),
+        travel(3, packed.at[1, first], final.at[0, first], right),
+        travel(4, packed.at[2, first], final.at[1, first], left),
+        travel(5, packed.at[2, second], final.at[1, second], left),
+    ]
+
+    def add(g, low, more=None):
+        @pl.loop(0, half)
+        def _(n):
+            term = partial[g, 1, low + n].astype(jnp.float32) + crossed[g, low + n].astype(jnp.float32)
+            if more is not None:
+                term += hop[more, n].astype(jnp.float32)
+            packed[g, low + n] = term.astype(jnp.bfloat16)
+
+    for g, steps in enumerate((2, 1, -1, 0)):
+        chip = lax.rem(z + steps + chips, chips)
+
+        @pl.loop(0, 2)
+        def _(turn):
+            attend(chip * 2 + lax.rem(core + 1 + turn, 2), turn)
+
+            @pl.loop(0, pieces)
+            def _(n):
+                partial[g, turn, n] = jnp.dot(
+                    attended[turn], projection[pl.ds(pl.multiple_of(n * width, width), width), :], preferred_element_type=jnp.float32
+                ).astype(jnp.bfloat16)
+
+            @pl.when(turn == 0)
+            def _():
+                cross(g).start()
+
+        cross(g).wait_recv()
+        if g == 0:
+            add(0, 0)
+            travels[0].start()
+            add(0, half)
+            travels[1].start()
+        elif g == 1:
+            add(1, half)
+            travels[2].start()
+        elif g == 2:
+            add(2, 0)
+            travels[4].start()
+            travels[0].wait_recv()
+            add(1, 0, 0)
+            travels[3].start()
+            travels[1].wait_recv()
+            add(2, half, 1)
+            travels[5].start()
+
+    for low, waits in ((half, (2, 5)), (0, (3, 4))):
+        for n in waits:
+            travels[n].wait_recv()
+
+        @pl.loop(0, half)
+        def _(n):
+            at = low + n
+            term = partial[3, 1, at].astype(jnp.float32) + crossed[3, at].astype(jnp.float32)
+            term += final[0, at].astype(jnp.float32) + final[1, at].astype(jnp.float32)
+            out[:, pl.ds(pl.multiple_of(at * wide, wide), wide)] = term.astype(jnp.bfloat16)
+
+    for g in range(chips):
+        cross(g).wait_send()
+    for copy in travels:
+        copy.wait_send()
 
     @pl.when(me < spans - 1)
     def _():
@@ -156,60 +429,51 @@
         def _():
             for copy in listed(me, me + step):
                 copy.wait_send()
-
-
-def exchange_and_attend(q, k, v, layout, spans):
-    rows, width = q.shape
+    for copy in sent:
+        copy.wait_send()
+
+
+def sublayer(tokens, norm_gain, qkv_weight, out_weight, layout, spans, lanes):
+    part, features = tokens.shape
+    width = qkv_weight.shape[2]
+    rows = lanes * part
     slots = 2 + layout.shape[1]
     pick, slot, reach = block_tables(layout, spans)
+    weights = jnp.concatenate([qkv_weight, out_weight[None]], axis=0)
     own = rows // BLK
     pool = own + CAP * spans + 1
-    q, k, v = (each.reshape(own, BLK, width) for each in (q, k, v))
+    whole = (spans, BLK, out_weight.shape[1])
     smem = pl.BlockSpec(memory_space=pltpu.SMEM)
     vmem = pl.BlockSpec(memory_space=pltpu.VMEM)
+    bf16 = lambda *shape: pltpu.VMEM(shape, jnp.bfloat16)
+    dma = lambda *shape: pltpu.SemaphoreType.DMA(shape)
+    side = math.isqrt(spans)
     return pl.pallas_call(
-        functools.partial(attend_kernel, spans, slots),
-        out_shape=jax.ShapeDtypeStruct((own, BLK, width), jnp.bfloat16),
+        functools.partial(attend_kernel, side, spans, slots),
+        out_shape=jax.ShapeDtypeStruct((BLK, features), jnp.bfloat16),
         in_specs=[smem] * 3 + [vmem] * 3,
         out_specs=vmem,
         scratch_shapes=[
-            pltpu.VMEM((pool, BLK, width), jnp.bfloat16),
-            pltpu.VMEM((pool, BLK, width), jnp.bfloat16),
-            pltpu.VMEM((spans * CAP, BLK, width), jnp.bfloat16),
-            pltpu.VMEM((spans * CAP, BLK, width), jnp.bfloat16),
-            pltpu.VMEM((slots, BLK, BLK), jnp.float32),
-            pltpu.SemaphoreType.DMA((2,)),
-            pltpu.SemaphoreType.DMA((spans + 1, 2)),
-            pltpu.SemaphoreType.DMA((spans + 1, 2)),
+            bf16(rows, features), bf16(rows, features), bf16(4, features, width), bf16(3, own, BLK, width),
+            bf16(pool, BLK, width), bf16(pool, BLK, width), bf16(spans * CAP, BLK, width), bf16(spans * CAP, BLK, width),
+            pltpu.VMEM((slots, BLK, BLK), jnp.float32), bf16(2, BLK, width),
+            bf16(4, 2, *whole), bf16(4, *whole), bf16(3, *whole), bf16(2, spans // 2, *whole[1:]), bf16(2, *whole),
+            dma(14), dma(lanes, 2), dma(60), dma(spans, 4), dma(2),
+            dma(spans + 1, 2), dma(spans + 1, 2), dma(2, 4), dma(6), dma(6),
         ],
         compiler_params=pltpu.CompilerParams(
-            collective_id=0, has_side_effects=True, vmem_limit_bytes=48 * 2**20
+            collective_id=0, has_side_effects=True, vmem_limit_bytes=67043328
         ),
-    )(pick, slot, reach, q, k, v).reshape(rows, width)
-
-
-def shards(spans, tokens, norm_gain, qkv_weight, out_weight, layout):
-    normed = normalize(tokens, norm_gain)
-    gathered = lax.all_gather(normed, "fsdp", axis=0, tiled=True)
-    projected = jnp.einsum(
-        "td,cdi->cti",
-        gathered,
-        lax.all_gather(qkv_weight, "ctx", axis=1, tiled=True),
-        preferred_element_type=jnp.float32,
-    ).astype(jnp.bfloat16)
-    attended = exchange_and_attend(projected[0], projected[1], projected[2], layout, spans)
-    projection = lax.all_gather(out_weight, "ctx", axis=1, tiled=True)
-    return lax.psum_scatter(
-        jnp.dot(attended, projection, preferred_element_type=jnp.float32).astype(jnp.bfloat16),
-        "fsdp",
-        scatter_dimension=0,
-        tiled=True,
-    )
+    )(pick, slot, reach, tokens, norm_gain[None, :], weights)
+
+
+def shards(spans, lanes, tokens, norm_gain, qkv_weight, out_weight, layout):
+    return sublayer(tokens, norm_gain, qkv_weight, out_weight, layout, spans, lanes)
 
 
 def solution(mesh):
     placed = (P(("ctx", "fsdp"), None), P(), P(None, "ctx", "fsdp"), P("fsdp", "ctx"), P())
     return jax.shard_map(
-        functools.partial(shards, mesh.shape["ctx"]),
+        functools.partial(shards, mesh.shape["ctx"], mesh.shape["fsdp"]),
         mesh=mesh, in_specs=placed, out_specs=P(("ctx", "fsdp"), None), check_vma=False,
     )

time: 294 us -> 183 us (0.62)
  waiting for transfers between devices: 173 us -> 0 us
  Pallas kernels: 82.2 us -> 173 us
  matrix products: 18.1 us -> 0 us
  between operations: 13.2 us -> 0.08 us
  local copies, waits for them, and re-layouts: 2.04 us -> 6.73 us
    all_gather x3 -> x0, waiting for transfers between devices: 118 us -> none  [the longest x1 56.5 us: shards(): lax.all_gather(qkv_weight, 'ctx', axis=1, tiled=True)]
    pallas_call x1, Pallas kernels: 82.2 us -> 173 us  [sublayer(): pl.pallas_call(functools.partial(attend_kernel, side, spans, slots), out_...]
    reduce_scatter x1 -> x0, waiting for transfers between devices: 54.3 us -> none  [shards(): lax.psum_scatter(jnp.dot(attended, projection, preferred_element_type=jnp...]
    dot_general x2 -> x0, matrix products: 18.1 us -> none  [the longest x1 10.9 us: shards(): jnp.einsum('td,cdi->cti', gathered, lax.all_gather(qkv_weight, 'ctx', axi...]
    unnamed x5 -> x6, local copies, waits for them, and re-layouts: 0.11 us -> 3.09 us
  transfers between devices with their start and end apart: 4 -> 0, of which waited for: 4 -> 0; matrix products, arithmetic and copies ran while one was open for 6% -> 0% of each run, Pallas kernels for 28% -> 0%
where the time goes in v5:
time: 183 us; the launch traced here: 182 us
  Pallas kernels  173 us (95%)
  local copies, waits for them, and re-layouts  6.73 us (4%)
  other arithmetic  2.5 us (1%)
    pallas_call x1, Pallas kernels, sublayer(): pl.pallas_call(functools.partial(attend_kernel, side, spans, slots), out_...  173 us

profile of v5, /device:TPU:30, one launch (start us, length us, event | category | flops | bytes accessed | tf_op | source)
XLA Modules:
  0.0 182.3 jit_solution(13608089315853000029)
XLA Ops:
  0.0 0.0 copy-start.1
  0.0 0.7 copy-done.1
  0.8 0.1 reduce_min.28
  0.8 0.1 reduce_min.29
  1.0 0.1 reduce_max.14
  1.1 0.1 reduce_max.18
  1.2 0.0 copy-start
  1.2 0.1 copy.9
  1.3 0.6 reshape.79.pick
  1.9 0.1 copy.10
  2.0 0.1 reshape.80
  2.1 0.5 broadcast.223
  2.6 0.7 fusion.7
  3.3 0.2 select_reduce_fusion
  3.5 0.1 reduce_min.31
  3.6 0.1 squeeze.6
  3.7 0.1 broadcast_subtract_fusion
  3.7 0.1 pad_add_fusion
  3.8 0.7 reshape.81.slot
  4.5 0.7 mul.25.reach
  5.2 0.0 copy-done
  5.2 1.8 %pad_maximum_fusion.weights = bf16[4,256,256]{2,1,0:T(8,128)(2,1)} fusion(bf16[1,256,256]{2,1,0:T(8,128)(2,1)S(1)} %bitcast.16, bf16[3,256,256]{2,1,0:T(8,128)(2,1)} %param.7), kind=kLoop, calls=%fused_computation | loop fusion | flops 262144 | bytes 1048576 | tf_op jit(solution)/shard_map/concatenate | solution.py:442
  7.0 173.0 %shard_map.55 = bf16[128,4096]{1,0:T(8,128)(2,1)} custom-call(s32[32]{0:T(128)} %reshape.79.pick, s32[144]{0:T(256)} %reshape.81.slot, s32[144]{0:T(256)} %mul.25.reach, bf16[128,4096]{1,0:T(8,128)(2,1)} %tokens.1, f32[1,4096]{1,0:T(1,128)} %bitcast.17, bf16[4,256,256]{2,1,0:T(8,128)(2,1)} %pad_maximum_fusion.weights), custom_call_target="tpu_custom_call" | custom-call | tf_op jit(solution)/shard_map/pallas_call | solution.py:451
  180.0 2.3 %copy.12 = bf16[128,4096]{1,0:T(8,128)(2,1)} copy(bf16[128,4096]{1,0:T(8,128)(2,1)} %shard_map.55) | data formatting | bytes 2097152
  (9 shorter events, 0.1 us)
Async XLA Ops:
  0.0 0.7 copy-start.1
  1.2 4.0 %copy-start = (bf16[256,256]{1,0:T(8,128)(2,1)S(1)}, bf16[256,256]{1,0:T(8,128)(2,1)}, u32[]{:S(2)}) copy-start(bf16[256,256]{1,0:T(8,128)(2,1)} %param.8) | copy-start | bytes 393220

commit v6 on v5

--- a/solution.py
+++ b/solution.py
@@ -291,12 +291,17 @@
         for copy in previous(me + 1):
             copy.start()
 
-    @pl.loop(1, spans)
-    def _(step):
-        @pl.when(me + step < spans)
-        def _():
-            for copy in listed(me, me + step):
-                copy.start()
+    x, y = me // side, lax.rem(me, side)
+    for by in (2, 3, 1, 0):
+
+        @pl.loop(0, side)
+        def _(step):
+            dst = (x + by) * side + lax.rem(y + step, side)
+
+            @pl.when((x + by < side) & (dst > me))
+            def _():
+                for copy in listed(me, dst):
+                    copy.start()
 
     project(0)
     for copy in keep:
@@ -314,27 +319,33 @@
             for copy in listed(me - step, me):
                 copy.wait_recv()
 
-    offset = lax.broadcasted_iota(jnp.int32, (BLK, BLK), 1) - lax.broadcasted_iota(jnp.int32, (BLK, BLK), 0)
+    column = lax.broadcasted_iota(jnp.int32, (BLK, 2 * BLK), 1)
+    late = column >= BLK
+    offset = lax.rem(column, BLK) - lax.broadcasted_iota(jnp.int32, (BLK, 2 * BLK), 0)
 
     def attend(b, at):
         for head in range(heads):
             columns = pl.ds(head * HEAD_DIM, HEAD_DIM)
             query = q[b, :, columns]
-            top = jnp.full((BLK, BLK), -1e30, jnp.float32)
-            for n in range(slots):
-                keys = kpool[slot[b * slots + n], :, columns]
-                part = lax.dot_general(query, keys, (((1,), (1,)), ((), ())), preferred_element_type=jnp.float32)
-                part = jnp.where(offset <= reach[b * slots + n], part * HEAD_DIM**-0.5, -1e30)
-                scores[n] = part
+            pair = lambda pool, n: jnp.concatenate(
+                [pool[slot[b * slots + n], :, columns], pool[slot[b * slots + n + 1], :, columns]], axis=0
+            )
+            top = jnp.full((BLK, 2 * BLK), -1e30, jnp.float32)
+            for n in range(0, slots, 2):
+                part = lax.dot_general(
+                    query, pair(kpool, n), (((1,), (1,)), ((), ())), preferred_element_type=jnp.float32
+                )
+                limit = jnp.where(late, reach[b * slots + n + 1], reach[b * slots + n])
+                part = jnp.where(offset <= limit, part, -1e30)
+                scores[n // 2] = part
                 top = jnp.maximum(top, part)
             top = jnp.max(top, axis=1, keepdims=True)
-            total = jnp.zeros((BLK, BLK), jnp.float32)
+            total = jnp.zeros((BLK, 2 * BLK), jnp.float32)
             blended = jnp.zeros((BLK, HEAD_DIM), jnp.float32)
-            for n in range(slots):
-                weights = jnp.exp(scores[n] - top)
-                total += weights
-                values = vpool[slot[b * slots + n], :, columns]
-                blended += jnp.dot(weights.astype(jnp.bfloat16), values, preferred_element_type=jnp.float32)
+            for n in range(0, slots, 2):
+                terms = jnp.exp((scores[n // 2] - top) * HEAD_DIM**-0.5)
+                total += terms
+                blended += jnp.dot(terms.astype(jnp.bfloat16), pair(vpool, n), preferred_element_type=jnp.float32)
             total = jnp.sum(total, axis=1, keepdims=True)
             attended[at, :, columns] = (blended / total).astype(jnp.bfloat16)
 
@@ -456,7 +467,7 @@
         scratch_shapes=[
             bf16(rows, features), bf16(rows, features), bf16(4, features, width), bf16(3, own, BLK, width),
             bf16(pool, BLK, width), bf16(pool, BLK, width), bf16(spans * CAP, BLK, width), bf16(spans * CAP, BLK, width),
-            pltpu.VMEM((slots, BLK, BLK), jnp.float32), bf16(2, BLK, width),
+            pltpu.VMEM((slots // 2, BLK, 2 * BLK), jnp.float32), bf16(2, BLK, width),
             bf16(4, 2, *whole), bf16(4, *whole), bf16(3, *whole), bf16(2, spans // 2, *whole[1:]), bf16(2, *whole),
             dma(14), dma(lanes, 2), dma(60), dma(spans, 4), dma(2),
             dma(spans + 1, 2), dma(spans + 1, 2), dma(2, 4), dma(6), dma(6),

time: 183 us -> 172 us (0.940)
  the two profiles are of different devices: /device:TPU:30 before, /device:TPU:18 now
where the time goes in v6:
time: 172 us
  Pallas kernels  162 us (94%)
  local copies, waits for them, and re-layouts  6.73 us (4%)
  other arithmetic  2.5 us (1%)
    pallas_call x1, Pallas kernels, sublayer(): pl.pallas_call(functools.partial(attend_kernel, side, spans, slots), out_...  162 us

profile of v6, /device:TPU:18, one launch (start us, length us, event | category | flops | bytes accessed | tf_op | source)
XLA Modules:
  0.0 171.6 jit_solution(4979326637108998555)
XLA Ops:
  0.0 0.0 copy-start.1
  0.0 0.7 copy-done.1
  0.8 0.1 reduce_min.28
  0.8 0.1 reduce_min.29
  1.0 0.1 reduce_max.14
  1.1 0.1 reduce_max.18
  1.2 0.0 copy-start
  1.2 0.1 copy.9
  1.3 0.6 reshape.79.pick
  1.9 0.1 copy.10
  2.0 0.1 reshape.80
  2.1 0.5 broadcast.223
  2.6 0.7 fusion.7
  3.3 0.2 select_reduce_fusion
  3.5 0.1 reduce_min.31
  3.6 0.1 squeeze.6
  3.7 0.1 broadcast_subtract_fusion
  3.7 0.1 pad_add_fusion
  3.8 0.7 reshape.81.slot
  4.5 0.7 mul.25.reach
  5.2 0.0 copy-done
  5.2 1.8 %pad_maximum_fusion.weights = bf16[4,256,256]{2,1,0:T(8,128)(2,1)} fusion(bf16[1,256,256]{2,1,0:T(8,128)(2,1)S(1)} %bitcast.16, bf16[3,256,256]{2,1,0:T(8,128)(2,1)} %param.7), kind=kLoop, calls=%fused_computation | loop fusion | flops 262144 | bytes 1048576 | tf_op jit(solution)/shard_map/concatenate | solution.py:453
  7.0 162.3 %shard_map.55 = bf16[128,4096]{1,0:T(8,128)(2,1)} custom-call(s32[32]{0:T(128)} %reshape.79.pick, s32[144]{0:T(256)} %reshape.81.slot, s32[144]{0:T(256)} %mul.25.reach, bf16[128,4096]{1,0:T(8,128)(2,1)} %tokens.1, f32[1,4096]{1,0:T(1,128)} %bitcast.17, bf16[4,256,256]{2,1,0:T(8,128)(2,1)} %pad_maximum_fusion.weights), custom_call_target="tpu_custom_call" | custom-call | tf_op jit(solution)/shard_map/pallas_call | solution.py:462
  169.3 2.3 %copy.12 = bf16[128,4096]{1,0:T(8,128)(2,1)} copy(bf16[128,4096]{1,0:T(8,128)(2,1)} %shard_map.55) | data formatting | bytes 2097152
  (9 shorter events, 0.1 us)
Async XLA Ops:
  0.0 0.7 copy-start.1
  1.2 4.0 %copy-start = (bf16[256,256]{1,0:T(8,128)(2,1)S(1)}, bf16[256,256]{1,0:T(8,128)(2,1)}, u32[]{:S(2)}) copy-start(bf16[256,256]{1,0:T(8,128)(2,1)} %param.8) | copy-start | bytes 393220

commit v7 on v6

--- a/solution.py
+++ b/solution.py
@@ -41,7 +41,7 @@
     return pick.astype(jnp.int32), slot.reshape(-1).astype(jnp.int32), reach.reshape(-1).astype(jnp.int32)
 
 
-def gather(side, eps, enter, tokens, gain, weights, rows_all, normed, held, send_t, recv_t, send_w, recv_w, own_sem):
+def gather(side, eps, enter, tokens, gain, weights, out_weight, rows_all, normed, held, projection, send_t, recv_t, send_w, recv_w, own_sem):
     ctx, lane = lax.axis_index("ctx"), lax.axis_index("fsdp")
     x, y = ctx // side, lax.rem(ctx, side)
     z, core = lane // 2, lax.rem(lane, 2)
@@ -78,21 +78,28 @@
             there, there, send_t.at[0], recv_t.at[owner, h], device_id=along("core", 1), device_id_type=MESH
         ).wait_recv()
 
-    def piece_of(owner, p):
-        return held.at[:, pl.ds(pl.multiple_of(owner * depth + p * quarter, quarter), quarter)]
-
-    def send_weights(owner, p, peer, own=False):
-        there = piece_of(owner, p)
-        here = weights.at[:, pl.ds(p * quarter, quarter)] if own else there
+    def rows_of(ref, start, count):
+        return ref.at[:, pl.ds(start, count)] if len(ref.shape) == 3 else ref.at[pl.ds(start, count)]
+
+    families = ((weights, held), (out_weight, projection))
+
+    def piece_of(owner, p, kind):
+        return rows_of(families[kind][1], pl.multiple_of(owner * depth + p * quarter, quarter), quarter)
+
+    def send_weights(owner, p, peer, kind=0, own=False):
+        there = piece_of(owner, p, kind)
+        here = rows_of(families[kind][0], p * quarter, quarter) if own else there
         copy = pltpu.make_async_remote_copy(
-            here, there, send_w.at[len([c for c in sent if c[0] == "w"])], recv_w.at[owner, p], device_id=peer, device_id_type=MESH
+            here, there, send_w.at[kind, len([c for c in sent if c[0] == kind])], recv_w.at[kind, owner, p],
+            device_id=peer, device_id_type=MESH,
         )
         copy.start()
-        sent.append(("w", copy))
-
-    def wait_weights(owner, p):
+        sent.append((kind, copy))
+
+    def wait_weights(owner, p, kind=0):
+        piece = piece_of(owner, p, kind)
         pltpu.make_async_remote_copy(
-            piece_of(owner, p), piece_of(owner, p), send_w.at[0], recv_w.at[owner, p], device_id=along("core", 1), device_id_type=MESH
+            piece, piece, send_w.at[kind, 0], recv_w.at[kind, owner, p], device_id=along("core", 1), device_id_type=MESH
         ).wait_recv()
 
     def normalize_rows(owner):
@@ -106,6 +113,7 @@
     keep = [
         pltpu.make_async_copy(tokens, rows_all.at[pl.ds(pl.multiple_of(lane * part, part), part)], own_sem.at[0]),
         pltpu.make_async_copy(weights, held.at[:, pl.ds(pl.multiple_of(ctx * depth, depth), depth)], own_sem.at[1]),
+        pltpu.make_async_copy(out_weight, projection.at[pl.ds(pl.multiple_of(ctx * depth, depth), depth)], own_sem.at[2]),
     ]
     for copy in keep:
         copy.start()
@@ -122,55 +130,66 @@
     lane_at = lambda by, flip=0: shift(z, by) * 2 + (1 - core if flip else core)
     send_tokens(lane, 0, right, own=True)
     send_tokens(lane, 1, left, own=True)
-    for first, second, p in routes:
-        send_weights(ctx, p, along(first, 1), own=True)
-        send_weights(ctx, p + 1, along(first, -1), own=True)
-        send_weights(ctx, p + 1, along(first, 1), own=True)
-        send_weights(ctx, p, along(first, -1), own=True)
+
+    def send_own(turn, kind=0):
+        for route in routes:
+            axis, p = route[turn], route[2]
+            send_weights(ctx, p, along(axis, 1), kind, own=True)
+            send_weights(ctx, p + 1, along(axis, -1), kind, own=True)
+            send_weights(ctx, p + 1, along(axis, 1), kind, own=True)
+            send_weights(ctx, p, along(axis, -1), kind, own=True)
+
+    send_own(0)
     send_tokens(lane, 1, right, own=True)
     send_tokens(lane, 0, left, own=True)
     for h in range(2):
         send_tokens(lane, h, sibling, own=True)
-    for first, second, p in routes:
-        send_weights(ctx, p, along(second, 1), own=True)
-        send_weights(ctx, p + 1, along(second, -1), own=True)
-        send_weights(ctx, p + 1, along(second, 1), own=True)
-        send_weights(ctx, p, along(second, -1), own=True)
+    send_own(1)
     for copy in keep:
         copy.wait()
     normalize_rows(lane)
 
-    def spread(owner, p, axis):
-        send_weights(owner, p, along(axis, 1))
-        send_weights(owner, p, along(axis, -1))
-
-    for first, second, p in routes:
-        wait_weights(owner_at(first, -1), p)
-        send_weights(owner_at(first, -1), p, along(first, 1))
-        wait_weights(owner_at(first, 1), p + 1)
-        send_weights(owner_at(first, 1), p + 1, along(first, -1))
-    for first, second, p in routes:
-        spread(owner_at(first, -1), p, second)
-        spread(owner_at(first, 1), p + 1, second)
-    for first, second, p in routes:
-        wait_weights(owner_at(first, -1), p + 1)
-        spread(owner_at(first, -1), p + 1, second)
-        wait_weights(owner_at(first, 1), p)
-        spread(owner_at(first, 1), p, second)
-
-    def relay(by):
+    def spread(owner, p, axis, kind):
+        send_weights(owner, p, along(axis, 1), kind)
+        send_weights(owner, p, along(axis, -1), kind)
+
+    def turn_corner(kind=0):
+        for first, second, p in routes:
+            wait_weights(owner_at(first, -1), p, kind)
+            send_weights(owner_at(first, -1), p, along(first, 1), kind)
+            wait_weights(owner_at(first, 1), p + 1, kind)
+            send_weights(owner_at(first, 1), p + 1, along(first, -1), kind)
+        for first, second, p in routes:
+            spread(owner_at(first, -1), p, second, kind)
+            spread(owner_at(first, 1), p + 1, second, kind)
+        for first, second, p in routes:
+            wait_weights(owner_at(first, -1), p + 1, kind)
+            spread(owner_at(first, -1), p + 1, second, kind)
+            wait_weights(owner_at(first, 1), p, kind)
+            spread(owner_at(first, 1), p, second, kind)
+        for first, second, p in routes:
+            for q in (p, p + 1):
+                wait_weights(owner_at(first, 2), q, kind)
+                spread(owner_at(first, 2), q, second, kind)
+
+    def relay(by, kind=0):
         for first, second, p in routes:
             owner = owner_at(first, by, -1)
-            wait_weights(owner, p)
-            send_weights(owner, p, along(second, 1))
+            wait_weights(owner, p, kind)
+            send_weights(owner, p, along(second, 1), kind)
             owner = owner_at(first, by, 1)
-            wait_weights(owner, p + 1)
-            send_weights(owner, p + 1, along(second, -1))
-
-    for first, second, p in routes:
-        for q in (p, p + 1):
-            wait_weights(owner_at(first, 2), q)
-            spread(owner_at(first, 2), q, second)
+            wait_weights(owner, p + 1, kind)
+            send_weights(owner, p + 1, along(second, -1), kind)
+
+    def finish(kind=0):
+        for first, second, p in routes:
+            for by in (0, -1, 1, 2):
+                wait_weights(owner_at(first, by, -1), p + 1, kind)
+                wait_weights(owner_at(first, by, 1), p, kind)
+                wait_weights(owner_at(first, by, 2), p, kind)
+                wait_weights(owner_at(first, by, 2), p + 1, kind)
+
+    turn_corner()
     relay(0)
     wait_tokens(lane_at(-1), 0)
     send_tokens(lane_at(-1), 0, right)
@@ -190,6 +209,8 @@
     normalize_rows(lane_at(-1))
     normalize_rows(lane_at(1))
     relay(2)
+    send_own(0, 1)
+    send_own(1, 1)
     for by in (-1, 1):
         for h in range(2):
             wait_tokens(lane_at(by, 1), h)
@@ -198,21 +219,17 @@
         wait_tokens(lane_at(2), h)
         send_tokens(lane_at(2), h, sibling)
     normalize_rows(lane_at(2))
-    for first, second, p in routes:
-        for by in (0, -1, 1, 2):
-            wait_weights(owner_at(first, by, -1), p + 1)
-            wait_weights(owner_at(first, by, 1), p)
-            wait_weights(owner_at(first, by, 2), p)
-            wait_weights(owner_at(first, by, 2), p + 1)
+    finish()
+    turn_corner(1)
     for h in range(2):
         wait_tokens(lane_at(2, 1), h)
     normalize_rows(lane_at(2, 1))
 
-    return [copy for _, copy in sent]
+    return sent, lambda *steps: [relay(by, 1) for by in steps], lambda: finish(1)
 
 
 def attend_kernel(
-    side, spans, slots, pick, slot, reach, tokens, gain, weights, out, rows_all, normed, held, projected,
+    side, spans, slots, pick, slot, reach, tokens, gain, weights, out_weight, out, rows_all, normed, held, projection, projected,
     kpool, vpool, kstage, vstage, scores, attended, partial, crossed, packed, hop, final,
     send_t, recv_t, send_w, recv_w, own_sem, send_sem, recv_sem, cross_sem, sum_send, sum_recv,
 ):
@@ -221,7 +238,6 @@
     z, core = lane // 2, lax.rem(lane, 2)
     chips = 4
     pieces, wide = spans, held.shape[2]
-    projection = held.at[3]
     half = pieces // 2
     right = (me, lax.rem(z + 1, chips) * 2 + core)
     left = (me, lax.rem(z + chips - 1, chips) * 2 + core)
@@ -239,9 +255,9 @@
     for peer in (right, left, sibling):
         pl.semaphore_signal(barrier, inc=1, device_id=peer, device_id_type=MESH)
 
-    sent = gather(
-        side, EPSILON, lambda: pl.semaphore_wait(barrier, spans + 2), tokens, gain, weights,
-        rows_all, normed, held, send_t, recv_t, send_w, recv_w, own_sem,
+    sent, relay_projection, finish_projection = gather(
+        side, EPSILON, lambda: pl.semaphore_wait(barrier, spans + 2), tokens, gain, weights, out_weight,
+        rows_all, normed, held, projection, send_t, recv_t, send_w, recv_w, own_sem,
     )
     tile = 2 * BLK
 
@@ -253,7 +269,9 @@
             projected[which, pl.ds(2 * n, 2)] = product.astype(jnp.bfloat16).reshape(2, BLK, width)
 
     project(1)
+    relay_projection(0, -1, 1)
     project(2)
+    relay_projection(2)
     keep = [
         pltpu.make_async_copy(k, kpool.at[pl.ds(0, own)], own_sem.at[0]),
         pltpu.make_async_copy(v, vpool.at[pl.ds(0, own)], own_sem.at[1]),
@@ -304,6 +322,7 @@
                     copy.start()
 
     project(0)
+    finish_projection()
     for copy in keep:
         copy.wait()
 
@@ -440,7 +459,7 @@
         def _():
             for copy in listed(me, me + step):
                 copy.wait_send()
-    for copy in sent:
+    for _, copy in sent:
         copy.wait_send()
 
 
@@ -450,7 +469,6 @@
     rows = lanes * part
     slots = 2 + layout.shape[1]
     pick, slot, reach = block_tables(layout, spans)
-    weights = jnp.concatenate([qkv_weight, out_weight[None]], axis=0)
     own = rows // BLK
     pool = own + CAP * spans + 1
     whole = (spans, BLK, out_weight.shape[1])
@@ -462,20 +480,21 @@
     return pl.pallas_call(
         functools.partial(attend_kernel, side, spans, slots),
         out_shape=jax.ShapeDtypeStruct((BLK, features), jnp.bfloat16),
-        in_specs=[smem] * 3 + [vmem] * 3,
+        in_specs=[smem] * 3 + [vmem] * 4,
         out_specs=vmem,
         scratch_shapes=[
-            bf16(rows, features), bf16(rows, features), bf16(4, features, width), bf16(3, own, BLK, width),
+            bf16(rows, features), bf16(rows, features), bf16(3, features, width), bf16(features, width),
+            bf16(3, own, BLK, width),
             bf16(pool, BLK, width), bf16(pool, BLK, width), bf16(spans * CAP, BLK, width), bf16(spans * CAP, BLK, width),
             pltpu.VMEM((slots // 2, BLK, 2 * BLK), jnp.float32), bf16(2, BLK, width),
             bf16(4, 2, *whole), bf16(4, *whole), bf16(3, *whole), bf16(2, spans // 2, *whole[1:]), bf16(2, *whole),
-            dma(14), dma(lanes, 2), dma(60), dma(spans, 4), dma(2),
+            dma(14), dma(lanes, 2), dma(2, 60), dma(2, spans, 4), dma(3),
             dma(spans + 1, 2), dma(spans + 1, 2), dma(2, 4), dma(6), dma(6),
         ],
         compiler_params=pltpu.CompilerParams(
             collective_id=0, has_side_effects=True, vmem_limit_bytes=67043328
         ),
-    )(pick, slot, reach, tokens, norm_gain[None, :], weights)
+    )(pick, slot, reach, tokens, norm_gain[None, :], qkv_weight, out_weight)
 
 
 def shards(spans, lanes, tokens, norm_gain, qkv_weight, out_weight, layout):

time: 172 us -> 167 us (0.971)
  Pallas kernels: 162 us -> 159 us
  other arithmetic: 2.5 us -> 0.67 us
    pallas_call x1, Pallas kernels: 162 us -> 159 us  [sublayer(): pl.pallas_call(functools.partial(attend_kernel, side, spans, slots), out_...]
    concatenate x1 -> x0, other arithmetic: 1.83 us -> none  [sublayer(): weights = jnp.concatenate([qkv_weight, out_weight[None]], axis=0)]
where the time goes in v7:
time: 167 us
  Pallas kernels  159 us (95%)
  local copies, waits for them, and re-layouts  6.67 us (4%)
    pallas_call x1, Pallas kernels, sublayer(): pl.pallas_call(functools.partial(attend_kernel, side, spans, slots), out_...  159 us

profile of v7, /device:TPU:18, one launch (start us, length us, event | category | flops | bytes accessed | tf_op | source)
XLA Modules:
  0.0 166.6 jit_solution(5162735252452368579)
XLA Ops:
  0.0 0.0 copy-start
  0.0 0.7 copy-done
  0.8 0.1 reduce_min.28
  0.8 0.1 reduce_min.29
  1.0 0.1 reduce_max.14
  1.1 0.1 reduce_max.18
  1.2 0.1 copy.9
  1.3 0.6 reshape.79.pick
  1.9 0.1 copy.10
  2.0 0.1 reshape.80
  2.1 0.5 broadcast.223
  2.6 0.7 fusion.7
  3.3 0.2 select_reduce_fusion
  3.5 0.1 reduce_min.31
  3.5 0.1 squeeze.6
  3.6 0.1 broadcast_subtract_fusion
  3.7 0.1 pad_add_fusion
  3.8 0.7 reshape.81.slot
  4.4 0.7 mul.25.reach
  5.1 159.2 %shard_map.55 = bf16[128,4096]{1,0:T(8,128)(2,1)} custom-call(s32[32]{0:T(128)} %reshape.79.pick, s32[144]{0:T(256)} %reshape.81.slot, s32[144]{0:T(256)} %mul.25.reach, bf16[128,4096]{1,0:T(8,128)(2,1)} %tokens.1, f32[1,4096]{1,0:T(1,128)} %bitcast.15, bf16[3,256,256]{2,1,0:T(8,128)(2,1)} %weights.1, bf16[256,256]{1,0:T(8,128)(2,1)} %out_weight.1), custom_call_target="tpu_custom_call" | custom-call | tf_op jit(solution)/shard_map/pallas_call | solution.py:480
  164.3 2.3 %copy.12 = bf16[128,4096]{1,0:T(8,128)(2,1)} copy(bf16[128,4096]{1,0:T(8,128)(2,1)} %shard_map.55) | data formatting | bytes 2097152
  (9 shorter events, 0.1 us)
Async XLA Ops:
  0.0 0.7 copy-start

commit v8 on v7

--- a/solution.py
+++ b/solution.py
@@ -19,26 +19,28 @@
     me = lax.axis_index("ctx")
     blocks, listed = layout.shape
     own = blocks // spans
-    entries = layout.reshape(spans, own * listed)
+    entries = layout.reshape(spans, own, listed)
     home, within = entries // own, entries % own
     mine = home == me
-    lowest = jnp.min(jnp.where(mine, within, own - 1), axis=1)
-    highest = jnp.max(jnp.where(mine, within, 0), axis=1)
-    pick = jnp.stack([lowest, highest], axis=1).reshape(-1)
-    rows = lax.dynamic_index_in_dim(entries, me, 0, keepdims=False)
+    lowest = jnp.min(jnp.where(mine, within, own - 1), axis=(1, 2))
+    highest = jnp.max(jnp.where(mine, within, 0), axis=(1, 2))
+    pick = jnp.stack([lowest, highest])
+    span = jnp.arange(spans, dtype=jnp.int32)
+    rows = jnp.sum(jnp.where(span[:, None, None] == me, entries, 0), axis=0)
     row_home, row_within = rows // own, rows % own
-    same = row_home[:, None] == row_home[None, :]
-    low = jnp.min(jnp.where(same, row_within[None, :], own - 1), axis=1)
+    from_span = row_home[:, :, None] == span
+    lows = jnp.min(jnp.where(from_span, row_within[:, :, None], own - 1), axis=(0, 1))
+    low = jnp.sum(jnp.where(from_span, lows, 0), axis=2)
     far = own + CAP * row_home + jnp.where(row_within == low, 0, 1)
-    listed_slot = jnp.where(row_home == me, row_within, far).reshape(own, listed)
+    listed_slot = jnp.where(row_home == me, row_within, far)
     index = jnp.arange(own, dtype=jnp.int32)
     block = me * own + index
     before = jnp.where(index > 0, index - 1, jnp.where(me > 0, own + CAP * spans, 0))
     slot = jnp.concatenate([index[:, None], before[:, None], listed_slot], axis=1)
-    gap = block[:, None] - rows.reshape(own, listed)
+    gap = block[:, None] - rows
     before_gap = jnp.where(block > 0, 1, -1)
     reach = jnp.concatenate([jnp.zeros_like(index)[:, None], before_gap[:, None], gap], axis=1) * BLK
-    return pick.astype(jnp.int32), slot.reshape(-1).astype(jnp.int32), reach.reshape(-1).astype(jnp.int32)
+    return pick.astype(jnp.int32), slot.astype(jnp.int32), reach.astype(jnp.int32)
 
 
 def gather(side, eps, enter, tokens, gain, weights, out_weight, rows_all, normed, held, projection, send_t, recv_t, send_w, recv_w, own_sem):
@@ -268,59 +270,55 @@
             product = jnp.dot(rows, held[which], preferred_element_type=jnp.float32)
             projected[which, pl.ds(2 * n, 2)] = product.astype(jnp.bfloat16).reshape(2, BLK, width)
 
+    x, y = me // side, lax.rem(me, side)
+    exchanged = ((k, kstage, kpool), (v, vstage, vpool))
+
+    def listed(j, src, dst):
+        _, stage, pool = exchanged[j]
+        return pltpu.make_async_remote_copy(
+            stage.at[pl.ds(CAP * dst, CAP)], pool.at[pl.ds(own + CAP * src, CAP)],
+            send_sem.at[dst, j], recv_sem.at[src, j], device_id=(dst, lane), device_id_type=MESH,
+        )
+
+    def previous(j, dst):
+        mine, _, pool = exchanged[j]
+        return pltpu.make_async_remote_copy(
+            mine.at[own - 1], pool.at[own + CAP * spans],
+            send_sem.at[spans, j], recv_sem.at[spans, j], device_id=(dst, lane), device_id_type=MESH,
+        )
+
+    def exchange(j):
+        mine, stage, pool = exchanged[j]
+        keep = pltpu.make_async_copy(mine, pool.at[pl.ds(0, own)], own_sem.at[j])
+        keep.start()
+
+        @pl.loop(0, spans)
+        def _(dst):
+            for which in range(CAP):
+                stage[CAP * dst + which] = mine[pick[which, dst]]
+
+        for by in (2, 3, 1, 0):
+
+            @pl.loop(0, side)
+            def _(step):
+                dst = (x + by) * side + lax.rem(y + step, side)
+
+                @pl.when((x + by < side) & (dst > me))
+                def _():
+                    listed(j, me, dst).start()
+
+        @pl.when(me < spans - 1)
+        def _():
+            previous(j, me + 1).start()
+
+        return keep
+
     project(1)
     relay_projection(0, -1, 1)
+    keep = [exchange(0)]
     project(2)
     relay_projection(2)
-    keep = [
-        pltpu.make_async_copy(k, kpool.at[pl.ds(0, own)], own_sem.at[0]),
-        pltpu.make_async_copy(v, vpool.at[pl.ds(0, own)], own_sem.at[1]),
-    ]
-    for copy in keep:
-        copy.start()
-
-    @pl.loop(0, spans * CAP)
-    def _(n):
-        kstage[n] = k[pick[n]]
-        vstage[n] = v[pick[n]]
-
-    def listed(src, dst):
-        there = pl.ds(own + CAP * src, CAP)
-        return [
-            pltpu.make_async_remote_copy(
-                stage.at[pl.ds(CAP * dst, CAP)], pool.at[there],
-                send_sem.at[dst, j], recv_sem.at[src, j], device_id=(dst, lane), device_id_type=MESH,
-            )
-            for j, (stage, pool) in enumerate(((kstage, kpool), (vstage, vpool)))
-        ]
-
-    def previous(dst):
-        there = own + CAP * spans
-        return [
-            pltpu.make_async_remote_copy(
-                mine.at[own - 1], pool.at[there],
-                send_sem.at[spans, j], recv_sem.at[spans, j], device_id=(dst, lane), device_id_type=MESH,
-            )
-            for j, (mine, pool) in enumerate(((k, kpool), (v, vpool)))
-        ]
-
-    @pl.when(me < spans - 1)
-    def _():
-        for copy in previous(me + 1):
-            copy.start()
-
-    x, y = me // side, lax.rem(me, side)
-    for by in (2, 3, 1, 0):
-
-        @pl.loop(0, side)
-        def _(step):
-            dst = (x + by) * side + lax.rem(y + step, side)
-
-            @pl.when((x + by < side) & (dst > me))
-            def _():
-                for copy in listed(me, dst):
-                    copy.start()
-
+    keep.append(exchange(1))
     project(0)
     finish_projection()
     for copy in keep:
@@ -328,15 +326,15 @@
 
     @pl.when(me > 0)
     def _():
-        for copy in previous(me):
-            copy.wait_recv()
+        for j in range(2):
+            previous(j, me).wait_recv()
 
     @pl.loop(1, spans)
     def _(step):
         @pl.when(me >= step)
         def _():
-            for copy in listed(me - step, me):
-                copy.wait_recv()
+            for j in range(2):
+                listed(j, me - step, me).wait_recv()
 
     column = lax.broadcasted_iota(jnp.int32, (BLK, 2 * BLK), 1)
     late = column >= BLK
@@ -347,14 +345,14 @@
             columns = pl.ds(head * HEAD_DIM, HEAD_DIM)
             query = q[b, :, columns]
             pair = lambda pool, n: jnp.concatenate(
-                [pool[slot[b * slots + n], :, columns], pool[slot[b * slots + n + 1], :, columns]], axis=0
+                [pool[slot[b, n], :, columns], pool[slot[b, n + 1], :, columns]], axis=0
             )
             top = jnp.full((BLK, 2 * BLK), -1e30, jnp.float32)
             for n in range(0, slots, 2):
                 part = lax.dot_general(
                     query, pair(kpool, n), (((1,), (1,)), ((), ())), preferred_element_type=jnp.float32
                 )
-                limit = jnp.where(late, reach[b * slots + n + 1], reach[b * slots + n])
+                limit = jnp.where(late, reach[b, n + 1], reach[b, n])
                 part = jnp.where(offset <= limit, part, -1e30)
                 scores[n // 2] = part
                 top = jnp.maximum(top, part)
@@ -450,15 +448,15 @@
 
     @pl.when(me < spans - 1)
     def _():
-        for copy in previous(me + 1):
-            copy.wait_send()
+        for j in range(2):
+            previous(j, me + 1).wait_send()
 
     @pl.loop(1, spans)
     def _(step):
         @pl.when(me + step < spans)
         def _():
-            for copy in listed(me, me + step):
-                copy.wait_send()
+            for j in range(2):
+                listed(j, me, me + step).wait_send()
     for _, copy in sent:
         copy.wait_send()
 

time: 167 us -> 163 us (0.976)
  the two profiles are of different devices: /device:TPU:18 before, /device:TPU:2 now
where the time goes in v8:
time: 163 us
  Pallas kernels  157 us (96%)
  local copies, waits for them, and re-layouts  3.24 us (2%)
  other arithmetic  2.16 us (1%)
    pallas_call x1, Pallas kernels, sublayer(): pl.pallas_call(functools.partial(attend_kernel, side, spans, slots), out_...  157 us

profile of v8, /device:TPU:2, one launch (start us, length us, event | category | flops | bytes accessed | tf_op | source)
XLA Modules:
  0.0 163.0 jit_solution(6341682083791985143)
XLA Ops:
  0.0 0.0 copy-start
  0.0 0.7 copy-done
  0.8 0.1 reduce_min.26
  0.8 0.1 reduce_min.27
  1.0 0.1 reduce_max.14
  1.1 0.1 reduce_max.18
  1.2 0.6 pad_add_fusion.1.pick
  1.8 0.1 copy.7
  1.9 0.1 fusion
  2.0 0.1 select_reduce_fusion.1
  2.1 0.3 select_reduce_fusion
  2.4 0.1 broadcast_subtract_fusion
  2.5 0.7 pad_add_fusion
  3.2 157.5 %shard_map.55 = bf16[128,4096]{1,0:T(8,128)(2,1)} custom-call(s32[2,16]{1,0:T(2,128)} %pad_add_fusion.1.pick, s32[8,18]{1,0:T(8,128)} %get-tuple-element.11.slot, s32[8,18]{1,0:T(8,128)} %get-tuple-element.12.reach, bf16[128,4096]{1,0:T(8,128)(2,1)} %tokens.1, f32[1,4096]{1,0:T(1,128)} %bitcast.7, bf16[3,256,256]{2,1,0:T(8,128)(2,1)} %weights.1, ...), custom_call_target="tpu_custom_call" | custom-call | tf_op jit(solution)/shard_map/pallas_call | solution.py:478
  160.7 2.3 %copy.9 = bf16[128,4096]{1,0:T(8,128)(2,1)} copy(bf16[128,4096]{1,0:T(8,128)(2,1)} %shard_map.55) | data formatting | bytes 2097152
  (8 shorter events, 0.1 us)
Async XLA Ops:
  0.0 0.7 copy-start
